TPU v7x, 32 devices: a whole 2x2x4 slice. The times are simulated.
32 devices in a mesh: groups: 2 (over x), pool: 2 (over core), tensor: 8 (over z, y).
Axes of the slice: x: 2, y: 2, z: 4, core: 2. Of those that a mesh axis runs over, the one named last changes fastest.
Arguments:
- rows: bfloat16 [512, 8192], P(('groups', 'pool', 'tensor')), parts along dimension 0, may hold values from -6 to 6
- norm_gain: float32 [8192], replicated, may hold values from 0.1 to 1.9
- w_query: bfloat16 [8192, 8192], P(None, ('pool', 'tensor')), may hold values from -0.0625 to 0.0625
- w_keyval: bfloat16 [8192, 2048], P(None, ('pool', 'tensor')), may hold values from -0.125 to 0.125
- w_out: bfloat16 [8192, 8192], P(('pool', 'tensor')), may hold values from -0.25 to 0.25
- key_cache: bfloat16 [512, 256, 1024], P(('groups', 'pool', 'tensor')), parts along dimension 0, may hold values from -104 to 104
- value_cache: bfloat16 [512, 256, 1024], P(('groups', 'pool', 'tensor')), parts along dimension 0, may hold values from -6 to 6
- lengths: int32 [512], P('groups'), parts along dimension 0, may hold values from 1 to 256, as said below
- slot_of: int32 [512], P('groups'), parts along dimension 0, may hold values from 0 to 255, each once
Outputs:
- projected: bfloat16 [512, 8192], P(('groups', 'pool', 'tensor')), parts along dimension 0
There are 2 independent parts, one for each index of `groups`. A program takes and returns all parts, laid end to end along the dimension named above; an argument that names none is the same for every part. Nothing has to cross between parts.
Inputs may be any that keep to these rules, and one draw needn't show every extreme that they name: `slot_of`: slots 16 * i to 16 * (i + 1) - 1 lie on index i of pool+tensor; every slot belongs to exactly one request. `lengths`: some request has exactly 256 cached tokens.
All inputs are finite; a program needn't handle non-finite values.
Results may differ from a plain program's by a relative error of at most 0.024.
Values may be sent and summed in bfloat16 or wider, within the bound.
No kernel may reach another device: no remote copies, remote signals or barrier semaphores. Data moves between devices by JAX's collectives and lax.ppermute only.
A program may use at most 128 MiB of HBM per device.

v0:
```python
import jax
import jax.numpy as jnp
from jax import lax
from jax.experimental import pallas as pl
from jax.experimental.pallas import tpu as pltpu
from jax.sharding import PartitionSpec as P


HEADS = 64
KVH = 8
HD = 128
EPS = 1e-05
AXES = ("pool", "tensor")
MIB = 1 << 20
CHUNK = 64
GROUP = 4


def ring_order(size):
    return list(range(0, size, 2)) + list(range(size - 1, 0, -2))


def ring_pairs(size):
    ring = ring_order(size)
    return [
        (p * size + ring[k], p * size + ring[(k + 1 - 2 * p) % size])
        for p in range(2)
        for k in range(size)
    ]


def sibling_pairs(size):
    return [(p * size + t, (1 - p) * size + t) for p in range(2) for t in range(size)]


def norm_kernel(rows_ref, gain_ref, out_ref):
    x = rows_ref[...].astype(jnp.float32)
    mean = jnp.mean(x * x, axis=1, keepdims=True)
    out_ref[...] = (x * lax.rsqrt(mean + EPS) * gain_ref[...]).astype(jnp.bfloat16)


def norm(rows, gain):
    whole = pl.BlockSpec(memory_space=pltpu.VMEM)
    return pl.pallas_call(
        norm_kernel,
        in_specs=[whole] * 2,
        out_specs=whole,
        out_shape=jax.ShapeDtypeStruct(rows.shape, jnp.bfloat16),
        compiler_params=pltpu.CompilerParams(vmem_limit_bytes=8 * MIB),
        name="norm",
    )(*[pltpu.with_memory_space_constraint(x, pltpu.HBM) for x in (rows, gain.reshape(1, -1))])


def project_kernel(count, last, depth, *refs):
    blocks = refs[:count]
    wq_ref, wkv_ref = refs[count : count + 2]
    starts = range(0, wq_ref.shape[0], depth)
    if last:
        slots_ref, before_ref, out_ref, acc = refs[count + 2 :]
    else:
        out_ref, wq_held, wkv_held, acc, sems = refs[count + 2 :]
        copies = []
        for i, start in enumerate(starts):
            cut = pl.ds(start, depth)
            copies.append(
                [
                    pltpu.make_async_copy(wq_ref.at[cut], wq_held.at[cut], sems.at[0, i]),
                    pltpu.make_async_copy(wkv_ref.at[cut], wkv_held.at[cut], sems.at[1, i]),
                ]
            )
            for copy in copies[-1]:
                copy.start()
        wq_ref, wkv_ref = wq_held, wkv_held
    query_cols = wq_ref.shape[1]
    for i, start in enumerate(starts):
        cut = slice(start, start + depth)
        part = jnp.concatenate([b[:, cut] for b in blocks], axis=0)
        if not last:
            for copy in copies[i]:
                copy.wait()
        query = jnp.dot(part, wq_ref[cut, :], preferred_element_type=jnp.float32)
        keyval = jnp.dot(part, wkv_ref[cut, :], preferred_element_type=jnp.float32)
        if i == 0:
            acc[:, :query_cols] = query
            acc[:, query_cols:] = keyval
        else:
            acc[:, :query_cols] += query
            acc[:, query_cols:] += keyval
    if not last:
        out_ref[...] = acc[...].astype(jnp.bfloat16)
        return
    requests = slots_ref.shape[1]
    ids = lax.broadcasted_iota(jnp.int32, (requests, requests), 0)
    order = (slots_ref[...] == ids).astype(jnp.bfloat16)
    both = jnp.concatenate([before_ref[...], acc[...].astype(jnp.bfloat16)], axis=0)
    out_ref[...] = jnp.dot(order, both, preferred_element_type=jnp.float32).astype(jnp.bfloat16)


def project(blocks, weights, depth, slots=None, before=None):
    count = len(blocks)
    rows = sum(b.shape[0] for b in blocks)
    width = sum(w.shape[1] for w in weights)
    last = slots is not None
    whole = pl.BlockSpec(memory_space=pltpu.VMEM)
    place = pltpu.VMEM if last else pltpu.HBM
    operands = list(blocks) + [pltpu.with_memory_space_constraint(w, place) for w in weights]
    specs = [whole] * count + [whole if last else pl.BlockSpec(memory_space=pl.ANY)] * 2
    out_shape = [jax.ShapeDtypeStruct((slots.shape[1] if last else rows, width), jnp.bfloat16)]
    scratch = [pltpu.VMEM((rows, width), jnp.float32)]
    if last:
        operands += [slots, before]
        specs += [whole] * 2
    else:
        out_shape += [pltpu.VMEM(w.shape, w.dtype) for w in weights]
        scratch.append(pltpu.SemaphoreType.DMA((2, weights[0].shape[0] // depth)))
    return pl.pallas_call(
        lambda *refs: project_kernel(count, last, depth, *refs),
        in_specs=specs,
        out_specs=[whole] * len(out_shape),
        out_shape=out_shape,
        scratch_shapes=scratch,
        compiler_params=pltpu.CompilerParams(vmem_limit_bytes=16 * MIB),
    )(*operands)


def attend_kernel(query_cols, group, order_ref, len_ref, arrived_ref, keys_hbm, values_hbm, out_ref,
                  keys_ref, values_ref, full, packed, sems):
    slots, cached, kv_width = keys_ref.shape
    rows = arrived_ref.shape[0]
    devices = rows // slots
    per_dev = query_cols // HD
    kv_cols = arrived_ref.shape[1] - query_cols
    pieces = HD // kv_cols
    share = HEADS // KVH
    scale = HD ** (-0.5)
    chunk = min(cached, CHUNK)
    widths = range(chunk, cached + 1, chunk)

    def longest(g):
        return len_ref[order_ref[g * group + group - 1]]

    def for_width(g, act):
        most = longest(g)
        for width in widths:
            pl.when((most > width - chunk) & (most <= width))(lambda width=width: act(width))

    def copies(g, i, width):
        at = g * group + i
        s = order_ref[at]
        for which, src, dst in ((0, keys_hbm, keys_ref), (1, values_hbm, values_ref)):
            cut = pl.ds(0, width)
            yield pltpu.make_async_copy(src.at[s, cut], dst.at[at, cut], sems.at[which, at])

    def begin(g, _):
        def start(width):
            for i in range(group):
                for copy in copies(g, i, width):
                    copy.start()

        for_width(g, start)
        return 0

    lax.fori_loop(0, slots // group, begin, 0)

    for i in range(per_dev):
        full[i] = arrived_ref[:, i * HD : (i + 1) * HD].astype(jnp.float32)
    target = lax.broadcasted_iota(jnp.int32, (rows, rows), 0)
    source = lax.broadcasted_iota(jnp.int32, (rows, rows), 1)
    holder = ((target // slots) * per_dev // share) * pieces
    fresh = arrived_ref[:, query_cols:]
    for which in range(2):
        for i in range(pieces):
            wanted = (which * (devices // 2) + holder + i) * slots + target % slots
            pick = (source == wanted).astype(jnp.bfloat16)
            full[per_dev + which, :, i * kv_cols : (i + 1) * kv_cols] = jnp.dot(
                pick, fresh, preferred_element_type=jnp.float32
            )
    row = lax.broadcasted_iota(jnp.int32, (HEADS, 1), 0)
    kv_head = ((row % devices) * per_dev + row // devices) // share
    lane_head = lax.broadcasted_iota(jnp.int32, (HEADS, kv_width), 1) // HD
    block_mask = lane_head == kv_head

    def of_slot(s, i):
        return full[i, pl.ds(s, devices, stride=slots), :]

    def repeated(s, i):
        return jnp.concatenate([of_slot(s, i)] * per_dev, axis=0)

    def one_group(g, _):
        def run(width):
            for i in range(group):
                for copy in copies(g, i, width):
                    copy.wait()
            ids = [order_ref[g * group + i] for i in range(group)]
            position = lax.broadcasted_iota(jnp.int32, (HEADS, width), 1)
            scores, owns = [], []
            for i, s in enumerate(ids):
                q = jnp.concatenate([of_slot(s, j) for j in range(per_dev)], axis=0)
                wide = jnp.where(block_mask, jnp.concatenate([q] * KVH, axis=1), 0.0)
                scores.append(
                    lax.dot_general(
                        wide.astype(jnp.bfloat16),
                        keys_ref[g * group + i, :width, :],
                        (((1,), (1,)), ((), ())),
                        preferred_element_type=jnp.float32,
                    )
                )
                owns.append(jnp.sum(q * repeated(s, per_dev), axis=1, keepdims=True) * scale)
            probs, weights = [], []
            for i, s in enumerate(ids):
                sc = jnp.where(position < len_ref[s], scores[i] * scale, -1e30)
                top = jnp.maximum(jnp.max(sc, axis=1, keepdims=True), owns[i])
                pr = jnp.exp(sc - top)
                own_prob = jnp.exp(owns[i] - top)
                total = jnp.sum(pr, axis=1, keepdims=True) + own_prob
                probs.append(pr.astype(jnp.bfloat16))
                weights.append((own_prob.astype(jnp.bfloat16).astype(jnp.float32), total))
            for i, s in enumerate(ids):
                all_heads = jnp.dot(
                    probs[i],
                    values_ref[g * group + i, :width, :],
                    preferred_element_type=jnp.float32,
                )
                mine = all_heads[:, :HD]
                for k in range(1, KVH):
                    mine = jnp.where(kv_head == k, all_heads[:, k * HD : (k + 1) * HD], mine)
                own_low, total = weights[i]
                mine = (mine + own_low * repeated(s, per_dev + 1)) / total
                for j in range(per_dev):
                    packed[j, pl.ds(s, devices, stride=slots), :] = mine[
                        j * devices : (j + 1) * devices
                    ]

        for_width(g, run)
        return 0

    lax.fori_loop(0, slots // group, one_group, 0)
    for i in range(per_dev):
        out_ref[:, i * HD : (i + 1) * HD] = packed[i].astype(jnp.bfloat16)


def attend(order, slot_len, arrived, key_cache, value_cache, query_cols):
    slots = key_cache.shape[0]
    rows = arrived.shape[0]
    group = max(g for g in range(1, GROUP + 1) if slots % g == 0)
    whole = pl.BlockSpec(memory_space=pltpu.VMEM)
    return pl.pallas_call(
        lambda *refs: attend_kernel(query_cols, group, *refs),
        in_specs=[pl.BlockSpec(memory_space=pltpu.SMEM)] * 2
        + [whole]
        + [pl.BlockSpec(memory_space=pl.ANY)] * 2,
        out_specs=whole,
        out_shape=jax.ShapeDtypeStruct((rows, query_cols), jnp.bfloat16),
        scratch_shapes=[
            pltpu.VMEM(key_cache.shape, key_cache.dtype),
            pltpu.VMEM(value_cache.shape, value_cache.dtype),
            pltpu.VMEM((query_cols // HD + 2, rows, HD), jnp.float32),
            pltpu.VMEM((query_cols // HD, rows, HD), jnp.float32),
            pltpu.SemaphoreType.DMA((2, slots)),
        ],
        compiler_params=pltpu.CompilerParams(vmem_limit_bytes=32 * MIB),
        name="attend",
    )(
        order,
        slot_len,
        arrived,
        pltpu.with_memory_space_constraint(key_cache, pltpu.HBM),
        pltpu.with_memory_space_constraint(value_cache, pltpu.HBM),
    )


def output_kernel(cuts, cols, fetching, slots_ref, back_ref, w_ref, *outs):
    requests = back_ref.shape[0]
    ids = lax.broadcasted_iota(jnp.int32, (requests, slots_ref.shape[1]), 0)
    order = (slots_ref[...] == ids).astype(jnp.bfloat16)
    starts = range(0, w_ref.shape[1], cols)
    copies = []
    if fetching:
        held, sems = outs[len(cuts)], outs[len(cuts) + 1]
        for i, start in enumerate(starts):
            cut = pl.ds(start, cols)
            copies.append(pltpu.make_async_copy(w_ref.at[:, cut], held.at[:, cut], sems.at[i]))
            copies[-1].start()
        w_ref = held
    rows = lax.dot_general(
        order, back_ref[...], (((0,), (0,)), ((), ())), preferred_element_type=jnp.float32
    ).astype(jnp.bfloat16)
    for i, start in enumerate(starts):
        cut = slice(start, start + cols)
        if fetching:
            copies[i].wait()
        out = jnp.dot(rows, w_ref[:, cut], preferred_element_type=jnp.float32).astype(jnp.bfloat16)
        first = 0
        for size, ref in zip(cuts, outs[: len(cuts)], strict=True):
            ref[:, cut] = out[first : first + size]
            first += size


def output(cuts, slots_local, returned, w_out, cols, fetching):
    model = w_out.shape[1]
    whole = pl.BlockSpec(memory_space=pltpu.VMEM)
    out_shape = [jax.ShapeDtypeStruct((size, model), jnp.bfloat16) for size in cuts]
    if fetching:
        out_shape.append(pltpu.VMEM(w_out.shape, w_out.dtype))
    place = pltpu.HBM if fetching else pltpu.VMEM
    return pl.pallas_call(
        lambda *refs: output_kernel(cuts, cols, fetching, *refs),
        in_specs=[whole] * 2 + [pl.BlockSpec(memory_space=pl.ANY) if fetching else whole],
        out_specs=[whole] * len(out_shape),
        out_shape=out_shape,
        scratch_shapes=[pltpu.SemaphoreType.DMA((model // cols,))] if fetching else [],
        compiler_params=pltpu.CompilerParams(vmem_limit_bytes=12 * MIB),
    )(slots_local, returned, pltpu.with_memory_space_constraint(w_out, place))


def add_up_kernel(starts, extra, block, *refs):
    outs = refs[2 * len(starts) + extra :]
    arrivals = refs[2 * len(starts) : 2 * len(starts) + extra]
    for i, (start, out) in enumerate(zip(starts, outs, strict=True)):
        cut = slice(start, start + block)
        total = refs[2 * i][cut, :].astype(jnp.float32) + refs[2 * i + 1][cut, :].astype(jnp.float32)
        for arrived in arrivals:
            total += arrived[...].astype(jnp.float32)
        out[...] = total.astype(jnp.bfloat16)


def add_up(pieces, arrivals, block):
    operands = [x for own, got, _ in pieces for x in (own, got)] + list(arrivals)
    starts = [start for _, _, start in pieces]
    model = operands[0].shape[1]
    whole = pl.BlockSpec(memory_space=pltpu.VMEM)
    return pl.pallas_call(
        lambda *refs: add_up_kernel(starts, len(arrivals), block, *refs),
        in_specs=[whole] * len(operands),
        out_specs=[whole] * len(starts),
        out_shape=[jax.ShapeDtypeStruct((block, model), jnp.bfloat16)] * len(starts),
        compiler_params=pltpu.CompilerParams(vmem_limit_bytes=8 * MIB),
    )(*operands)


def body(rows, norm_gain, w_query, w_keyval, w_out, key_cache, value_cache, lengths, slot_of):
    size = lax.axis_size("tensor")
    devices = lax.axis_size(AXES)
    half = size // 2
    block = rows.shape[0]
    slots_dev = key_cache.shape[0]
    query_cols = w_query.shape[1]
    forward = lambda x: lax.ppermute(x, AXES, ring_pairs(size))
    swap = lambda x: lax.ppermute(x, AXES, sibling_pairs(size))

    pool = lax.axis_index("pool")
    tensor = lax.axis_index("tensor")
    way = 1 - 2 * pool
    place = jnp.where(tensor % 2 == 0, tensor // 2, size - 1 - tensor // 2)

    def device_at(steps, owner):
        at = (place + way * steps + 2 * size) % size
        return owner * size + jnp.where(at < half, 2 * at, 2 * (size - 1 - at) + 1)

    slot_blocks = slot_of.reshape(devices, block)

    def slots_in(order):
        pick = jnp.stack(order)[:, None] == jnp.arange(devices, dtype=jnp.int32)[None, :]
        return jnp.sum(jnp.where(pick[:, :, None], slot_blocks[None], 0), axis=1).reshape(-1)

    normed = norm(rows, norm_gain)
    a, b = normed, swap(normed)
    blocks, order = [a, b], [device_at(0, pool), device_at(0, 1 - pool)]
    late, late_order = [], []
    for k in range(1, half):
        a, b = forward(a), forward(b)
        blocks += [a, swap(a)]
        order += [device_at(-k, pool), device_at(k, 1 - pool)]
        into, into_order = (blocks, order) if k < half - 1 else (late, late_order)
        into += [b, swap(b)]
        into_order += [device_at(-k, 1 - pool), device_at(k, pool)]
    a = forward(a)
    late += [a, swap(a)]
    late_order += [device_at(-half, pool), device_at(half, 1 - pool)]

    own_slots = lax.axis_index(AXES) * slots_dev + jnp.arange(slots_dev, dtype=jnp.int32)
    slot_len = jnp.sum(
        jnp.where(slot_of[None, :] == own_slots[:, None], lengths[None, :], 0), axis=1
    )
    theirs, mine = [device_at(-half, 1 - pool)], [device_at(half, pool)]
    for k in range(half - 1, 0, -1):
        theirs += [device_at(-k, 1 - pool), device_at(-k, pool)]
        mine += [device_at(k, pool), device_at(k, 1 - pool)]
    theirs += [device_at(0, 1 - pool)]
    mine += [device_at(0, pool)]
    each = jnp.arange(slots_dev, dtype=jnp.int32)
    shorter = (slot_len[None, :] < slot_len[:, None]) | (
        (slot_len[None, :] == slot_len[:, None]) & (each[None, :] < each[:, None])
    )
    rank = jnp.sum(shorter.astype(jnp.int32), axis=1)
    by_length = jnp.sum(jnp.where(rank[None, :] == each[:, None], each[None, :], 0), axis=1)
    w_query, w_keyval, slot_len, by_length, slots_local, slots_early, slots_rest = (
        lax.optimization_barrier(
            (
                w_query,
                w_keyval,
                slot_len,
                by_length,
                slots_in(order + late_order).reshape(1, -1),
                slots_in(theirs + mine[:3]).reshape(1, -1),
                slots_in(mine[3:]).reshape(1, -1),
            )
        )
    )
    depth = w_query.shape[0] // 8
    early_rows, *weights = project(blocks, (w_query, w_keyval), depth)
    (sending,) = project(late, weights, depth, slots_local, early_rows)
    arrived = lax.all_to_all(sending, AXES, split_axis=0, concat_axis=0, tiled=True)

    attended = attend(by_length, slot_len, arrived, key_cache, value_cache, query_cols)
    returned = lax.all_to_all(attended, AXES, split_axis=0, concat_axis=0, tiled=True)
    early = 3 * block
    rest = block * len(mine) - early
    cols = w_out.shape[1] // 8
    first, later, own_first, held = output(
        (early, rest, early), slots_early, returned, w_out, cols, True
    )
    first, later = swap(first), swap(later)
    (own_later,) = output((rest,), slots_rest, returned, held, cols, False)

    def chip_sum(items, arrivals=()):
        pieces = [(own_first, first, i) if i < 3 else (own_later, later, i - 3) for i in items]
        return add_up([(o, g, at * block) for o, g, at in pieces], arrivals, block)

    a, b = chip_sum((0, 2))
    a = forward(a)
    b = forward(b)
    at = 1
    for k in range(half - 1, 0, -1):
        (a,) = chip_sum((at,), (a,))
        a = forward(a)
        if k > 1:
            (b,) = chip_sum((at + 3,), (b,))
            b = forward(b)
        at += 2
    across = swap(b)
    (out,) = chip_sum((at,), (a, across))
    return out


def solution(mesh):
    placed = (
        P(("groups", "pool", "tensor"), None),
        P(),
        P(None, ("pool", "tensor")),
        P(None, ("pool", "tensor")),
        P(("pool", "tensor"), None),
        P(("groups", "pool", "tensor"), None, None),
        P(("groups", "pool", "tensor"), None, None),
        P("groups"),
        P("groups"),
    )

    return jax.shard_map(
        body,
        mesh=mesh,
        in_specs=placed,
        out_specs=P(("groups", "pool", "tensor"), None),
        check_vma=False,
    )
```

profile of v0, /device:TPU:0, one launch (start us, length us, event | category | flops | bytes accessed | tf_op | source)
XLA Modules:
  0.0 113.0 jit_solution(1314768801188533657)
XLA Ops:
  0.0 1.2 %norm.1.refs_0_ = bf16[16,8192]{1,0:T(8,128)(2,1)S(1)} custom-call(bf16[16,8192]{1,0:T(8,128)(2,1)} %rows_ref.1, f32[1,8192]{1,0:T(1,128)} %bitcast.28), custom_call_target="tpu_custom_call" | custom-call | tf_op jit(solution)/shard_map/norm/pallas_call | solution.py:44
  1.2 3.1 %collective-permute-start.5 = (bf16[16,8192]{1,0:T(8,128)(2,1)S(1)}, bf16[16,8192]{1,0:T(8,128)(2,1)S(1)}, u32[]{:S(2)}, u32[]{:S(2)}) collective-permute-start(bf16[16,8192]{1,0:T(8,128)(2,1)S(1)} %norm.1.refs_0_), channel_id=1, source_target_pairs={{0,2},{2,4},{4,6},{6,7},{7,5},{5,3},{3,1},{1,0},{8,9},{10,8},{12,1... | collective-permute-start | bytes 786440 | tf_op jit(solution)/shard_map/ppermute | solution.py:348
  4.4 4.2 %collective-permute-done.5.refs_2_ = bf16[16,8192]{1,0:T(8,128)(2,1)S(1)} collective-permute-done((bf16[16,8192]{1,0:T(8,128)(2,1)S(1)}, bf16[16,8192]{1,0:T(8,128)(2,1)S(1)}, u32[]{:S(2)}, u32[]{:S(2)}) %collective-permute-start.5) | collective-permute-done | bytes 262176 | tf_op jit(solution)/shard_map/ppermute | solution.py:348
  8.6 2.1 %collective-permute-start.6 = (bf16[16,8192]{1,0:T(8,128)(2,1)S(1)}, bf16[16,8192]{1,0:T(8,128)(2,1)S(1)}, u32[]{:S(2)}, u32[]{:S(2)}) collective-permute-start(bf16[16,8192]{1,0:T(8,128)(2,1)S(1)} %collective-permute-done.5.refs_2_), channel_id=1, source_target_pairs={{0,2},{2,4},{4,6},{6,7},{7,5},{5,3},{3,1},{1,0},{8,9},{10,8},{12,1... | collective-permute-start | bytes 786440 | tf_op jit(solution)/shard_map/ppermute | solution.py:348
  10.7 1.6 %collective-permute-start.1 = (bf16[16,8192]{1,0:T(8,128)(2,1)S(1)}, bf16[16,8192]{1,0:T(8,128)(2,1)S(1)}, u32[]{:S(2)}, u32[]{:S(2)}) collective-permute-start(bf16[16,8192]{1,0:T(8,128)(2,1)S(1)} %collective-permute-done.refs_1_), channel_id=1, source_target_pairs={{0,2},{2,4},{4,6},{6,7},{7,5},{5,3},{3,1},{1,0},{8,9},{10,8},{12,1... | collective-permute-start | bytes 786440 | tf_op jit(solution)/shard_map/ppermute | solution.py:348
  12.3 0.8 broadcast_in_dim.109
  13.2 1.7 %collective-permute-done.6.refs_6_ = bf16[16,8192]{1,0:T(8,128)(2,1)S(1)} collective-permute-done((bf16[16,8192]{1,0:T(8,128)(2,1)S(1)}, bf16[16,8192]{1,0:T(8,128)(2,1)S(1)}, u32[]{:S(2)}, u32[]{:S(2)}) %collective-permute-start.6) | collective-permute-done | bytes 262176 | tf_op jit(solution)/shard_map/ppermute | solution.py:348
  15.0 2.1 %collective-permute-start.7 = (bf16[16,8192]{1,0:T(8,128)(2,1)S(1)}, bf16[16,8192]{1,0:T(8,128)(2,1)S(1)}, u32[]{:S(2)}, u32[]{:S(2)}) collective-permute-start(bf16[16,8192]{1,0:T(8,128)(2,1)S(1)} %collective-permute-done.6.refs_6_), channel_id=1, source_target_pairs={{0,2},{2,4},{4,6},{6,7},{7,5},{5,3},{3,1},{1,0},{8,9},{10,8},{12,1... | collective-permute-start | bytes 786440 | tf_op jit(solution)/shard_map/ppermute | solution.py:348
  17.0 0.7 collective-permute-done.1.refs_4_
  17.8 2.1 %collective-permute-start.2 = (bf16[16,8192]{1,0:T(8,128)(2,1)S(1)}, bf16[16,8192]{1,0:T(8,128)(2,1)S(1)}, u32[]{:S(2)}, u32[]{:S(2)}) collective-permute-start(bf16[16,8192]{1,0:T(8,128)(2,1)S(1)} %collective-permute-done.1.refs_4_), channel_id=1, source_target_pairs={{0,2},{2,4},{4,6},{6,7},{7,5},{5,3},{3,1},{1,0},{8,9},{10,8},{12,1... | collective-permute-start | bytes 786440 | tf_op jit(solution)/shard_map/ppermute | solution.py:348
  20.1 0.5 collective-permute-start.12
  20.6 0.7 collective-permute-done.7.refs_10_
  21.3 2.1 %collective-permute-start.8 = (bf16[16,8192]{1,0:T(8,128)(2,1)S(1)}, bf16[16,8192]{1,0:T(8,128)(2,1)S(1)}, u32[]{:S(2)}, u32[]{:S(2)}) collective-permute-start(bf16[16,8192]{1,0:T(8,128)(2,1)S(1)} %collective-permute-done.7.refs_10_), channel_id=1, source_target_pairs={{0,2},{2,4},{4,6},{6,7},{7,5},{5,3},{3,1},{1,0},{8,9},{10,8},{12,1... | collective-permute-start | bytes 786440 | tf_op jit(solution)/shard_map/ppermute | solution.py:348
  23.4 0.7 collective-permute-done.2.refs_8_
  24.1 2.1 %collective-permute-start.3 = (bf16[16,8192]{1,0:T(8,128)(2,1)S(1)}, bf16[16,8192]{1,0:T(8,128)(2,1)S(1)}, u32[]{:S(2)}, u32[]{:S(2)}) collective-permute-start(bf16[16,8192]{1,0:T(8,128)(2,1)S(1)} %collective-permute-done.2.refs_8_), channel_id=1, source_target_pairs={{0,2},{2,4},{4,6},{6,7},{7,5},{5,3},{3,1},{1,0},{8,9},{10,8},{12,1... | collective-permute-start | bytes 786440 | tf_op jit(solution)/shard_map/ppermute | solution.py:348
  26.2 0.1 select_reduce_fusion.1
  26.3 0.1 select_reduce_fusion
  26.5 0.5 collective-permute-start.14
  27.1 0.6 collective-permute-done.8.refs_2_
  27.7 2.8 %collective-permute-done.3.refs_0_ = bf16[16,8192]{1,0:T(8,128)(2,1)S(1)} collective-permute-done((bf16[16,8192]{1,0:T(8,128)(2,1)S(1)}, bf16[16,8192]{1,0:T(8,128)(2,1)S(1)}, u32[]{:S(2)}, u32[]{:S(2)}) %collective-permute-start.3) | collective-permute-done | bytes 262176 | tf_op jit(solution)/shard_map/ppermute | solution.py:348
  30.5 0.9 select_reduce_fusion.3.refs_1_
  31.6 0.2 convert_reduce_fusion
  31.8 0.1 select_reduce_fusion.4.refs_0_
  32.0 6.6 %shard_map.91 = (bf16[192,640]{1,0:T(8,128)(2,1)S(1)}, bf16[8192,512]{1,0:T(8,128)(2,1)S(1)}, bf16[8192,128]{1,0:T(8,128)(2,1)S(1)}) custom-call(bf16[16,8192]{1,0:T(8,128)(2,1)S(1)} %norm.1.refs_0_, bf16[16,8192]{1,0:T(8,128)(2,1)S(1)} %collective-permute-done.refs_1_, bf16[16,8192]{1,0:T(8,128)(2,1)S(1)} %collective-permute-done.5.refs_2_, ...), custom_call_target="tpu_custom_call" | custom-call | tf_op jit(solution)/shard_map/pallas_call | solution.py:116
  38.6 2.1 %shard_map.92 = bf16[256,640]{1,0:T(8,128)(2,1)S(1)} custom-call(bf16[16,8192]{1,0:T(8,128)(2,1)S(1)} %collective-permute-done.3.refs_0_, bf16[16,8192]{1,0:T(8,128)(2,1)S(1)} %collective-permute-done.4.refs_1_, bf16[16,8192]{1,0:T(8,128)(2,1)S(1)} %collective-permute-done.8.refs_2_, bf16[16,8192]{1,0:T(8,128)(2,1)S(1)} %collective-permute-done.9.refs_3_, ...), custom_call_target="tpu_custom_call" | custom-call | tf_op jit(solution)/shard_map/pallas_call | solution.py:116
  40.6 18.0 %all_to_all.22 = bf16[16,16,640]{2,1,0:T(8,128)(2,1)S(1)} all-to-all(bf16[16,16,640]{2,1,0:T(8,128)(2,1)S(1)} %bitcast.25), channel_id=1, replica_groups=mesh['groups'=2,'pool'=2,'tensor'=8] {'pool','tensor'}, dimensions={0} | all-to-all | bytes 655360 | tf_op jit(solution)/shard_map/all_to_all | solution.py:413
  58.7 5.1 %attend.1 = bf16[256,512]{1,0:T(8,128)(2,1)S(1)} custom-call(s32[16]{0:T(128)S(1)} %select_reduce_fusion.4.refs_0_, s32[16]{0:T(128)S(1)} %select_reduce_fusion.3.refs_1_, bf16[256,640]{1,0:T(8,128)(2,1)S(1)} %bitcast.26, bf16[16,256,1024]{2,1,0:T(8,128)(2,1)} %refs_3_.1, bf16[16,256,1024]{2,1,0:T(8,128)(2,1)} %refs_4_.1), custom_call_target="tpu_custom_call" | custom-call | tf_op jit(solution)/shard_map/attend/pallas_call | solution.py:247
  63.8 13.7 %all_to_all.23 = bf16[16,16,512]{2,1,0:T(8,128)(2,1)S(1)} all-to-all(bf16[16,16,512]{2,1,0:T(8,128)(2,1)S(1)} %bitcast.27), channel_id=1, replica_groups=mesh['groups'=2,'pool'=2,'tensor'=8] {'pool','tensor'}, dimensions={0} | all-to-all | bytes 524288 | tf_op jit(solution)/shard_map/all_to_all | solution.py:416
  77.5 4.3 %shard_map.93 = (bf16[48,8192]{1,0:T(8,128)(2,1)S(1)}, bf16[80,8192]{1,0:T(8,128)(2,1)S(1)}, bf16[48,8192]{1,0:T(8,128)(2,1)S(1)}, bf16[512,8192]{1,0:T(8,128)(2,1)S(1)}) custom-call(s32[1,176]{1,0:T(1,128)S(1)} %reshape_reshape.10.refs_0_, bf16[256,512]{1,0:T(8,128)(2,1)S(1)} %bitcast.23, bf16[512,8192]{1,0:T(8,128)(2,1)} %refs_2_.1), custom_call_target="tpu_custom_call" | custom-call | tf_op jit(solution)/shard_map/pallas_call | solution.py:306
  81.9 0.5 collective-permute-start.16
  82.4 3.6 %collective-permute-done.16.refs_1_.refs_3_ = bf16[48,8192]{1,0:T(8,128)(2,1)S(1)} collective-permute-done((bf16[48,8192]{1,0:T(8,128)(2,1)S(1)}, bf16[48,8192]{1,0:T(8,128)(2,1)S(1)}, u32[]{:S(2)}, u32[]{:S(2)}) %collective-permute-start.16) | collective-permute-done | bytes 786464 | tf_op jit(solution)/shard_map/ppermute | solution.py:349
  86.0 0.1 shard_map.95
  86.2 0.8 collective-permute-start.17
  87.0 1.7 %shard_map.94.refs_0_ = bf16[80,8192]{1,0:T(8,128)(2,1)S(1)} custom-call(s32[1,80]{1,0:T(1,128)S(1)} %reshape_reshape.11.refs_0_, bf16[256,512]{1,0:T(8,128)(2,1)S(1)} %bitcast.24, bf16[512,8192]{1,0:T(8,128)(2,1)S(1)} %get-tuple-element.31.refs_2_), custom_call_target="tpu_custom_call" | custom-call | tf_op jit(solution)/shard_map/pallas_call | solution.py:306
  88.7 3.8 %collective-permute-done.17.refs_2_ = bf16[16,8192]{1,0:T(8,128)(2,1)S(1)} collective-permute-done((bf16[16,8192]{1,0:T(8,128)(2,1)S(1)}, bf16[16,8192]{1,0:T(8,128)(2,1)S(1)}, u32[]{:S(2)}, u32[]{:S(2)}) %collective-permute-start.17) | collective-permute-done | bytes 262176 | tf_op jit(solution)/shard_map/ppermute | solution.py:348
  92.6 0.1 shard_map.96
  92.7 0.8 collective-permute-start.18
  93.5 1.9 %collective-permute-done.21.refs_2_ = bf16[16,8192]{1,0:T(8,128)(2,1)S(1)} collective-permute-done((bf16[16,8192]{1,0:T(8,128)(2,1)S(1)}, bf16[16,8192]{1,0:T(8,128)(2,1)S(1)}, u32[]{:S(2)}, u32[]{:S(2)}) %collective-permute-start.21) | collective-permute-done | bytes 262176 | tf_op jit(solution)/shard_map/ppermute | solution.py:348
  95.5 0.8 collective-permute-start.22
  96.3 2.8 %collective-permute-done.18.refs_2_ = bf16[16,8192]{1,0:T(8,128)(2,1)S(1)} collective-permute-done((bf16[16,8192]{1,0:T(8,128)(2,1)S(1)}, bf16[16,8192]{1,0:T(8,128)(2,1)S(1)}, u32[]{:S(2)}, u32[]{:S(2)}) %collective-permute-start.18) | collective-permute-done | bytes 262176 | tf_op jit(solution)/shard_map/ppermute | solution.py:348
  99.2 0.8 collective-permute-start.19
  100.0 1.9 %collective-permute-done.22.refs_2_ = bf16[16,8192]{1,0:T(8,128)(2,1)S(1)} collective-permute-done((bf16[16,8192]{1,0:T(8,128)(2,1)S(1)}, bf16[16,8192]{1,0:T(8,128)(2,1)S(1)}, u32[]{:S(2)}, u32[]{:S(2)}) %collective-permute-start.22) | collective-permute-done | bytes 262176 | tf_op jit(solution)/shard_map/ppermute | solution.py:348
  102.0 0.8 collective-permute-start.23
  102.8 2.8 %collective-permute-done.19.refs_2_ = bf16[16,8192]{1,0:T(8,128)(2,1)S(1)} collective-permute-done((bf16[16,8192]{1,0:T(8,128)(2,1)S(1)}, bf16[16,8192]{1,0:T(8,128)(2,1)S(1)}, u32[]{:S(2)}, u32[]{:S(2)}) %collective-permute-start.19) | collective-permute-done | bytes 262176 | tf_op jit(solution)/shard_map/ppermute | solution.py:348
  105.7 0.8 collective-permute-start.20
  106.5 1.9 %collective-permute-done.23 = bf16[16,8192]{1,0:T(8,128)(2,1)S(1)} collective-permute-done((bf16[16,8192]{1,0:T(8,128)(2,1)S(1)}, bf16[16,8192]{1,0:T(8,128)(2,1)S(1)}, u32[]{:S(2)}, u32[]{:S(2)}) %collective-permute-start.23) | collective-permute-done | bytes 262176 | tf_op jit(solution)/shard_map/ppermute | solution.py:348
  108.4 3.7 %collective-permute-done.20.refs_2_ = bf16[16,8192]{1,0:T(8,128)(2,1)S(1)} collective-permute-done((bf16[16,8192]{1,0:T(8,128)(2,1)S(1)}, bf16[16,8192]{1,0:T(8,128)(2,1)S(1)}, u32[]{:S(2)}, u32[]{:S(2)}) %collective-permute-start.20) | collective-permute-done | bytes 262176 | tf_op jit(solution)/shard_map/ppermute | solution.py:348
  112.2 0.8 shard_map.101
  (34 shorter events, 1.5 us)
Async XLA Ops:
  1.2 7.4 %collective-permute-start.5 = (bf16[16,8192]{1,0:T(8,128)(2,1)S(1)}, bf16[16,8192]{1,0:T(8,128)(2,1)S(1)}, u32[]{:S(2)}, u32[]{:S(2)}) collective-permute-start(bf16[16,8192]{1,0:T(8,128)(2,1)S(1)} %norm.1.refs_0_), channel_id=1, source_target_pairs={{0,2},{2,4},{4,6},{6,7},{7,5},{5,3},{3,1},{1,0},{8,9},{10,8},{12,1... | collective-permute-start | bytes 786440 | tf_op jit(solution)/shard_map/ppermute | solution.py:348
  4.3 6.4 %collective-permute-start = (bf16[16,8192]{1,0:T(8,128)(2,1)S(1)}, bf16[16,8192]{1,0:T(8,128)(2,1)S(1)}, u32[]{:S(2)}, u32[]{:S(2)}) collective-permute-start(bf16[16,8192]{1,0:T(8,128)(2,1)S(1)} %norm.1.refs_0_), channel_id=1, source_target_pairs={{0,8},{1,9},{2,10},{3,11},{4,12},{5,13},{6,14},{7,15},{8,0},{9,1},... | collective-permute-start | bytes 786440 | tf_op jit(solution)/shard_map/ppermute | solution.py:349
  8.6 6.4 %collective-permute-start.6 = (bf16[16,8192]{1,0:T(8,128)(2,1)S(1)}, bf16[16,8192]{1,0:T(8,128)(2,1)S(1)}, u32[]{:S(2)}, u32[]{:S(2)}) collective-permute-start(bf16[16,8192]{1,0:T(8,128)(2,1)S(1)} %collective-permute-done.5.refs_2_), channel_id=1, source_target_pairs={{0,2},{2,4},{4,6},{6,7},{7,5},{5,3},{3,1},{1,0},{8,9},{10,8},{12,1... | collective-permute-start | bytes 786440 | tf_op jit(solution)/shard_map/ppermute | solution.py:348
  10.7 7.1 %collective-permute-start.1 = (bf16[16,8192]{1,0:T(8,128)(2,1)S(1)}, bf16[16,8192]{1,0:T(8,128)(2,1)S(1)}, u32[]{:S(2)}, u32[]{:S(2)}) collective-permute-start(bf16[16,8192]{1,0:T(8,128)(2,1)S(1)} %collective-permute-done.refs_1_), channel_id=1, source_target_pairs={{0,2},{2,4},{4,6},{6,7},{7,5},{5,3},{3,1},{1,0},{8,9},{10,8},{12,1... | collective-permute-start | bytes 786440 | tf_op jit(solution)/shard_map/ppermute | solution.py:348
  15.0 6.4 %collective-permute-start.7 = (bf16[16,8192]{1,0:T(8,128)(2,1)S(1)}, bf16[16,8192]{1,0:T(8,128)(2,1)S(1)}, u32[]{:S(2)}, u32[]{:S(2)}) collective-permute-start(bf16[16,8192]{1,0:T(8,128)(2,1)S(1)} %collective-permute-done.6.refs_6_), channel_id=1, source_target_pairs={{0,2},{2,4},{4,6},{6,7},{7,5},{5,3},{3,1},{1,0},{8,9},{10,8},{12,1... | collective-permute-start | bytes 786440 | tf_op jit(solution)/shard_map/ppermute | solution.py:348
  17.8 6.4 %collective-permute-start.2 = (bf16[16,8192]{1,0:T(8,128)(2,1)S(1)}, bf16[16,8192]{1,0:T(8,128)(2,1)S(1)}, u32[]{:S(2)}, u32[]{:S(2)}) collective-permute-start(bf16[16,8192]{1,0:T(8,128)(2,1)S(1)} %collective-permute-done.1.refs_4_), channel_id=1, source_target_pairs={{0,2},{2,4},{4,6},{6,7},{7,5},{5,3},{3,1},{1,0},{8,9},{10,8},{12,1... | collective-permute-start | bytes 786440 | tf_op jit(solution)/shard_map/ppermute | solution.py:348
  20.1 6.4 %collective-permute-start.10 = (bf16[16,8192]{1,0:T(8,128)(2,1)S(1)}, bf16[16,8192]{1,0:T(8,128)(2,1)S(1)}, u32[]{:S(2)}, u32[]{:S(2)}) collective-permute-start(bf16[16,8192]{1,0:T(8,128)(2,1)S(1)} %collective-permute-done.5.refs_2_), channel_id=1, source_target_pairs={{0,8},{1,9},{2,10},{3,11},{4,12},{5,13},{6,14},{7,15},{8,0},{9,1},... | collective-permute-start | bytes 786440 | tf_op jit(solution)/shard_map/ppermute | solution.py:349
  20.1 6.9 %collective-permute-start.12 = (bf16[16,8192]{1,0:T(8,128)(2,1)S(1)}, bf16[16,8192]{1,0:T(8,128)(2,1)S(1)}, u32[]{:S(2)}, u32[]{:S(2)}) collective-permute-start(bf16[16,8192]{1,0:T(8,128)(2,1)S(1)} %collective-permute-done.6.refs_6_), channel_id=1, source_target_pairs={{0,8},{1,9},{2,10},{3,11},{4,12},{5,13},{6,14},{7,15},{8,0},{9,1},... | collective-permute-start | bytes 786440 | tf_op jit(solution)/shard_map/ppermute | solution.py:349
  21.3 6.4 %collective-permute-start.8 = (bf16[16,8192]{1,0:T(8,128)(2,1)S(1)}, bf16[16,8192]{1,0:T(8,128)(2,1)S(1)}, u32[]{:S(2)}, u32[]{:S(2)}) collective-permute-start(bf16[16,8192]{1,0:T(8,128)(2,1)S(1)} %collective-permute-done.7.refs_10_), channel_id=1, source_target_pairs={{0,2},{2,4},{4,6},{6,7},{7,5},{5,3},{3,1},{1,0},{8,9},{10,8},{12,1... | collective-permute-start | bytes 786440 | tf_op jit(solution)/shard_map/ppermute | solution.py:348
  24.1 6.4 %collective-permute-start.3 = (bf16[16,8192]{1,0:T(8,128)(2,1)S(1)}, bf16[16,8192]{1,0:T(8,128)(2,1)S(1)}, u32[]{:S(2)}, u32[]{:S(2)}) collective-permute-start(bf16[16,8192]{1,0:T(8,128)(2,1)S(1)} %collective-permute-done.2.refs_8_), channel_id=1, source_target_pairs={{0,2},{2,4},{4,6},{6,7},{7,5},{5,3},{3,1},{1,0},{8,9},{10,8},{12,1... | collective-permute-start | bytes 786440 | tf_op jit(solution)/shard_map/ppermute | solution.py:348
  26.5 5.5 %collective-permute-start.11 = (bf16[16,8192]{1,0:T(8,128)(2,1)S(1)}, bf16[16,8192]{1,0:T(8,128)(2,1)}, u32[]{:S(2)}, u32[]{:S(2)}) collective-permute-start(bf16[16,8192]{1,0:T(8,128)(2,1)S(1)} %collective-permute-done.1.refs_4_), channel_id=1, source_target_pairs={{0,8},{1,9},{2,10},{3,11},{4,12},{5,13},{6,14},{7,15},{8,0},{9,1},... | collective-permute-start | bytes 786440 | tf_op jit(solution)/shard_map/ppermute | solution.py:349
  26.5 5.4 %collective-permute-start.14 = (bf16[16,8192]{1,0:T(8,128)(2,1)S(1)}, bf16[16,8192]{1,0:T(8,128)(2,1)}, u32[]{:S(2)}, u32[]{:S(2)}) collective-permute-start(bf16[16,8192]{1,0:T(8,128)(2,1)S(1)} %collective-permute-done.7.refs_10_), channel_id=1, source_target_pairs={{0,8},{1,9},{2,10},{3,11},{4,12},{5,13},{6,14},{7,15},{8,0},{9,1},... | collective-permute-start | bytes 786440 | tf_op jit(solution)/shard_map/ppermute | solution.py:349
  27.0 4.9 %collective-permute-start.13 = (bf16[16,8192]{1,0:T(8,128)(2,1)S(1)}, bf16[16,8192]{1,0:T(8,128)(2,1)}, u32[]{:S(2)}, u32[]{:S(2)}) collective-permute-start(bf16[16,8192]{1,0:T(8,128)(2,1)S(1)} %collective-permute-done.2.refs_8_), channel_id=1, source_target_pairs={{0,8},{1,9},{2,10},{3,11},{4,12},{5,13},{6,14},{7,15},{8,0},{9,1},... | collective-permute-start | bytes 786440 | tf_op jit(solution)/shard_map/ppermute | solution.py:349
  27.7 10.8 %collective-permute-start.9 = (bf16[16,8192]{1,0:T(8,128)(2,1)S(1)}, bf16[16,8192]{1,0:T(8,128)(2,1)S(1)}, u32[]{:S(2)}, u32[]{:S(2)}) collective-permute-start(bf16[16,8192]{1,0:T(8,128)(2,1)S(1)} %collective-permute-done.8.refs_2_), channel_id=1, source_target_pairs={{0,8},{1,9},{2,10},{3,11},{4,12},{5,13},{6,14},{7,15},{8,0},{9,1},... | collective-permute-start | bytes 786440 | tf_op jit(solution)/shard_map/ppermute | solution.py:349
  30.5 8.1 %collective-permute-start.4 = (bf16[16,8192]{1,0:T(8,128)(2,1)S(1)}, bf16[16,8192]{1,0:T(8,128)(2,1)S(1)}, u32[]{:S(2)}, u32[]{:S(2)}) collective-permute-start(bf16[16,8192]{1,0:T(8,128)(2,1)S(1)} %collective-permute-done.3.refs_0_), channel_id=1, source_target_pairs={{0,8},{1,9},{2,10},{3,11},{4,12},{5,13},{6,14},{7,15},{8,0},{9,1},... | collective-permute-start | bytes 786440 | tf_op jit(solution)/shard_map/ppermute | solution.py:349
  81.8 13.6 %collective-permute-start.15 = (bf16[80,8192]{1,0:T(8,128)(2,1)S(1)}, bf16[80,8192]{1,0:T(8,128)(2,1)S(1)}, u32[]{:S(2)}, u32[]{:S(2)}) collective-permute-start(bf16[80,8192]{1,0:T(8,128)(2,1)S(1)} %get-tuple-element.32), channel_id=1, source_target_pairs={{0,8},{1,9},{2,10},{3,11},{4,12},{5,13},{6,14},{7,15},{8,0},{9,1},... | collective-permute-start | bytes 3932168 | tf_op jit(solution)/shard_map/ppermute | solution.py:349
  81.9 4.1 %collective-permute-start.16 = (bf16[48,8192]{1,0:T(8,128)(2,1)S(1)}, bf16[48,8192]{1,0:T(8,128)(2,1)S(1)}, u32[]{:S(2)}, u32[]{:S(2)}) collective-permute-start(bf16[48,8192]{1,0:T(8,128)(2,1)S(1)} %get-tuple-element.34), channel_id=1, source_target_pairs={{0,8},{1,9},{2,10},{3,11},{4,12},{5,13},{6,14},{7,15},{8,0},{9,1},... | collective-permute-start | bytes 2359304 | tf_op jit(solution)/shard_map/ppermute | solution.py:349
  86.2 6.4 %collective-permute-start.17 = (bf16[16,8192]{1,0:T(8,128)(2,1)S(1)}, bf16[16,8192]{1,0:T(8,128)(2,1)S(1)}, u32[]{:S(2)}, u32[]{:S(2)}) collective-permute-start(bf16[16,8192]{1,0:T(8,128)(2,1)S(1)} %get-tuple-element.35), channel_id=1, source_target_pairs={{0,2},{2,4},{4,6},{6,7},{7,5},{5,3},{3,1},{1,0},{8,9},{10,8},{12,1... | collective-permute-start | bytes 786440 | tf_op jit(solution)/shard_map/ppermute | solution.py:348
  86.9 8.4 %collective-permute-start.21 = (bf16[16,8192]{1,0:T(8,128)(2,1)S(1)}, bf16[16,8192]{1,0:T(8,128)(2,1)S(1)}, u32[]{:S(2)}, u32[]{:S(2)}) collective-permute-start(bf16[16,8192]{1,0:T(8,128)(2,1)S(1)} %get-tuple-element.36), channel_id=1, source_target_pairs={{0,2},{2,4},{4,6},{6,7},{7,5},{5,3},{3,1},{1,0},{8,9},{10,8},{12,1... | collective-permute-start | bytes 786440 | tf_op jit(solution)/shard_map/ppermute | solution.py:348
  92.7 6.4 %collective-permute-start.18 = (bf16[16,8192]{1,0:T(8,128)(2,1)S(1)}, bf16[16,8192]{1,0:T(8,128)(2,1)S(1)}, u32[]{:S(2)}, u32[]{:S(2)}) collective-permute-start(bf16[16,8192]{1,0:T(8,128)(2,1)S(1)} %shard_map.96), channel_id=1, source_target_pairs={{0,2},{2,4},{4,6},{6,7},{7,5},{5,3},{3,1},{1,0},{8,9},{10,8},{12,1... | collective-permute-start | bytes 786440 | tf_op jit(solution)/shard_map/ppermute | solution.py:348
  95.5 6.4 %collective-permute-start.22 = (bf16[16,8192]{1,0:T(8,128)(2,1)S(1)}, bf16[16,8192]{1,0:T(8,128)(2,1)S(1)}, u32[]{:S(2)}, u32[]{:S(2)}) collective-permute-start(bf16[16,8192]{1,0:T(8,128)(2,1)S(1)} %shard_map.99), channel_id=1, source_target_pairs={{0,2},{2,4},{4,6},{6,7},{7,5},{5,3},{3,1},{1,0},{8,9},{10,8},{12,1... | collective-permute-start | bytes 786440 | tf_op jit(solution)/shard_map/ppermute | solution.py:348
  99.2 6.4 %collective-permute-start.19 = (bf16[16,8192]{1,0:T(8,128)(2,1)S(1)}, bf16[16,8192]{1,0:T(8,128)(2,1)S(1)}, u32[]{:S(2)}, u32[]{:S(2)}) collective-permute-start(bf16[16,8192]{1,0:T(8,128)(2,1)S(1)} %shard_map.97), channel_id=1, source_target_pairs={{0,2},{2,4},{4,6},{6,7},{7,5},{5,3},{3,1},{1,0},{8,9},{10,8},{12,1... | collective-permute-start | bytes 786440 | tf_op jit(solution)/shard_map/ppermute | solution.py:348
  102.0 6.4 %collective-permute-start.23 = (bf16[16,8192]{1,0:T(8,128)(2,1)S(1)}, bf16[16,8192]{1,0:T(8,128)(2,1)S(1)}, u32[]{:S(2)}, u32[]{:S(2)}) collective-permute-start(bf16[16,8192]{1,0:T(8,128)(2,1)S(1)} %shard_map.100), channel_id=1, source_target_pairs={{0,2},{2,4},{4,6},{6,7},{7,5},{5,3},{3,1},{1,0},{8,9},{10,8},{12,1... | collective-permute-start | bytes 786440 | tf_op jit(solution)/shard_map/ppermute | solution.py:348
  105.7 6.4 %collective-permute-start.20 = (bf16[16,8192]{1,0:T(8,128)(2,1)S(1)}, bf16[16,8192]{1,0:T(8,128)(2,1)S(1)}, u32[]{:S(2)}, u32[]{:S(2)}) collective-permute-start(bf16[16,8192]{1,0:T(8,128)(2,1)S(1)} %shard_map.98), channel_id=1, source_target_pairs={{0,2},{2,4},{4,6},{6,7},{7,5},{5,3},{3,1},{1,0},{8,9},{10,8},{12,1... | collective-permute-start | bytes 786440 | tf_op jit(solution)/shard_map/ppermute | solution.py:348
  108.4 3.7 %collective-permute-start.24 = (bf16[16,8192]{1,0:T(8,128)(2,1)S(1)}, bf16[16,8192]{1,0:T(8,128)(2,1)S(1)}, u32[]{:S(2)}, u32[]{:S(2)}) collective-permute-start(bf16[16,8192]{1,0:T(8,128)(2,1)S(1)} %collective-permute-done.23), channel_id=1, source_target_pairs={{0,8},{1,9},{2,10},{3,11},{4,12},{5,13},{6,14},{7,15},{8,0},{9,1},... | collective-permute-start | bytes 786440 | tf_op jit(solution)/shard_map/ppermute | solution.py:349
where the time goes:
time: 113 us
  waiting for transfers between devices  34.1 us (30%)
  blocking collectives  31.8 us (28%)
  Pallas kernels  22.4 us (20%)
  starting transfers between devices  21.6 us (19%)
  other arithmetic  1.7 us (2%)
  local copies, waits for them, and re-layouts  1.25 us (1%)
    ppermute x14, waiting for transfers between devices, body(): forward = lambda x: lax.ppermute(x, AXES, ring_pairs(size))  30.5 us
    ppermute x14, starting transfers between devices, body(): forward = lambda x: lax.ppermute(x, AXES, ring_pairs(size))  19.8 us
    all_to_all x1, blocking collectives, body(): lax.all_to_all(sending, AXES, split_axis=0, concat_axis=0, tiled=True)  18 us
    all_to_all x1, blocking collectives, body(): lax.all_to_all(attended, AXES, split_axis=0, concat_axis=0, tiled=True)  13.7 us
    pallas_call x2, Pallas kernels, project(): pl.pallas_call(lambda *refs: project_kernel(count, last, depth, *refs), i...  8.63 us
    pallas_call x2, Pallas kernels, output(): pl.pallas_call(lambda *refs: output_kernel(cuts, cols, fetching, *refs),...  5.99 us
    pallas_call x1, Pallas kernels, attend(): pl.pallas_call(lambda *refs: attend_kernel(query_cols, group, *refs), in_...  5.1 us
    ppermute x11, waiting for transfers between devices, body(): swap = lambda x: lax.ppermute(x, AXES, sibling_pairs(size))  3.68 us
  transfers between devices with their start and end apart: 25, of which 15 were waited for; matrix products, arithmetic and copies ran while one was open for 3% of the time, Pallas kernels for 8%

commit v1 on v0

--- a/solution.py
+++ b/solution.py
@@ -14,6 +14,7 @@
 MIB = 1 << 20
 CHUNK = 64
 GROUP = 4
+AHEAD = 3
 
 
 def ring_order(size):
@@ -56,7 +57,7 @@
     wq_ref, wkv_ref = refs[count : count + 2]
     starts = range(0, wq_ref.shape[0], depth)
     if last:
-        slots_ref, before_ref, out_ref, acc = refs[count + 2 :]
+        slots_ref, devices_ref, before_ref, out_ref, acc, in_order = refs[count + 2 :]
     else:
         out_ref, wq_held, wkv_held, acc, sems = refs[count + 2 :]
         copies = []
@@ -68,7 +69,8 @@
                     pltpu.make_async_copy(wkv_ref.at[cut], wkv_held.at[cut], sems.at[1, i]),
                 ]
             )
-            for copy in copies[-1]:
+        for some in copies[:AHEAD]:
+            for copy in some:
                 copy.start()
         wq_ref, wkv_ref = wq_held, wkv_held
     query_cols = wq_ref.shape[1]
@@ -78,6 +80,9 @@
         if not last:
             for copy in copies[i]:
                 copy.wait()
+            for some in copies[i + AHEAD : i + AHEAD + 1]:
+                for copy in some:
+                    copy.start()
         query = jnp.dot(part, wq_ref[cut, :], preferred_element_type=jnp.float32)
         keyval = jnp.dot(part, wkv_ref[cut, :], preferred_element_type=jnp.float32)
         if i == 0:
@@ -90,13 +95,23 @@
         out_ref[...] = acc[...].astype(jnp.bfloat16)
         return
     requests = slots_ref.shape[1]
+    block = blocks[0].shape[0]
+    early = before_ref.shape[0] // block
+    for i in range(requests // block):
+        at = pl.ds(pl.multiple_of(devices_ref[i] * block, block), block)
+        if i < early:
+            in_order[at, :] = before_ref[i * block : (i + 1) * block, :]
+        else:
+            cut = slice((i - early) * block, (i - early + 1) * block)
+            in_order[at, :] = acc[cut, :].astype(jnp.bfloat16)
     ids = lax.broadcasted_iota(jnp.int32, (requests, requests), 0)
-    order = (slots_ref[...] == ids).astype(jnp.bfloat16)
-    both = jnp.concatenate([before_ref[...], acc[...].astype(jnp.bfloat16)], axis=0)
-    out_ref[...] = jnp.dot(order, both, preferred_element_type=jnp.float32).astype(jnp.bfloat16)
-
-
-def project(blocks, weights, depth, slots=None, before=None):
+    to_slots = (slots_ref[...] == ids).astype(jnp.bfloat16)
+    out_ref[...] = jnp.dot(
+        to_slots, in_order[...], preferred_element_type=jnp.float32
+    ).astype(jnp.bfloat16)
+
+
+def project(blocks, weights, depth, slots=None, devices=None, before=None):
     count = len(blocks)
     rows = sum(b.shape[0] for b in blocks)
     width = sum(w.shape[1] for w in weights)
@@ -108,8 +123,9 @@
     out_shape = [jax.ShapeDtypeStruct((slots.shape[1] if last else rows, width), jnp.bfloat16)]
     scratch = [pltpu.VMEM((rows, width), jnp.float32)]
     if last:
-        operands += [slots, before]
-        specs += [whole] * 2
+        operands += [slots, devices, before]
+        specs += [whole, pl.BlockSpec(memory_space=pltpu.SMEM), whole]
+        scratch.append(pltpu.VMEM((slots.shape[1], width), jnp.bfloat16))
     else:
         out_shape += [pltpu.VMEM(w.shape, w.dtype) for w in weights]
         scratch.append(pltpu.SemaphoreType.DMA((2, weights[0].shape[0] // depth)))
@@ -160,7 +176,8 @@
         for_width(g, start)
         return 0
 
-    lax.fori_loop(0, slots // group, begin, 0)
+    groups = slots // group
+    lax.fori_loop(0, min(2, groups), begin, 0)
 
     for i in range(per_dev):
         full[i] = arrived_ref[:, i * HD : (i + 1) * HD].astype(jnp.float32)
@@ -191,6 +208,11 @@
             for i in range(group):
                 for copy in copies(g, i, width):
                     copy.wait()
+
+            @pl.when(g + 2 < groups)
+            def _():
+                begin(g + 2, 0)
+
             ids = [order_ref[g * group + i] for i in range(group)]
             position = lax.broadcasted_iota(jnp.int32, (HEADS, width), 1)
             scores, owns = [], []
@@ -234,7 +256,7 @@
         for_width(g, run)
         return 0
 
-    lax.fori_loop(0, slots // group, one_group, 0)
+    lax.fori_loop(0, groups, one_group, 0)
     for i in range(per_dev):
         out_ref[:, i * HD : (i + 1) * HD] = packed[i].astype(jnp.bfloat16)
 
@@ -269,10 +291,11 @@
     )
 
 
-def output_kernel(cuts, cols, fetching, slots_ref, back_ref, w_ref, *outs):
+def output_kernel(cuts, cols, block, first_block, fetching, slots_ref, devices_ref, back_ref, w_ref, *outs):
     requests = back_ref.shape[0]
-    ids = lax.broadcasted_iota(jnp.int32, (requests, slots_ref.shape[1]), 0)
-    order = (slots_ref[...] == ids).astype(jnp.bfloat16)
+    *outs, in_order = outs
+    ids = lax.broadcasted_iota(jnp.int32, (requests, requests), 0)
+    to_slots = (slots_ref[...] == ids).astype(jnp.bfloat16)
     starts = range(0, w_ref.shape[1], cols)
     copies = []
     if fetching:
@@ -280,15 +303,25 @@
         for i, start in enumerate(starts):
             cut = pl.ds(start, cols)
             copies.append(pltpu.make_async_copy(w_ref.at[:, cut], held.at[:, cut], sems.at[i]))
-            copies[-1].start()
+        for copy in copies[:AHEAD]:
+            copy.start()
         w_ref = held
-    rows = lax.dot_general(
-        order, back_ref[...], (((0,), (0,)), ((), ())), preferred_element_type=jnp.float32
+    in_order[...] = lax.dot_general(
+        to_slots, back_ref[...], (((0,), (0,)), ((), ())), preferred_element_type=jnp.float32
     ).astype(jnp.bfloat16)
+    rows = jnp.concatenate(
+        [
+            in_order[pl.ds(pl.multiple_of(devices_ref[first_block + i] * block, block), block), :]
+            for i in range(sum(cuts) // block)
+        ],
+        axis=0,
+    )
     for i, start in enumerate(starts):
         cut = slice(start, start + cols)
         if fetching:
             copies[i].wait()
+            for copy in copies[i + AHEAD : i + AHEAD + 1]:
+                copy.start()
         out = jnp.dot(rows, w_ref[:, cut], preferred_element_type=jnp.float32).astype(jnp.bfloat16)
         first = 0
         for size, ref in zip(cuts, outs[: len(cuts)], strict=True):
@@ -296,7 +329,7 @@
             first += size
 
 
-def output(cuts, slots_local, returned, w_out, cols, fetching):
+def output(cuts, block, first_block, slots, devices, returned, w_out, cols, fetching):
     model = w_out.shape[1]
     whole = pl.BlockSpec(memory_space=pltpu.VMEM)
     out_shape = [jax.ShapeDtypeStruct((size, model), jnp.bfloat16) for size in cuts]
@@ -304,13 +337,15 @@
         out_shape.append(pltpu.VMEM(w_out.shape, w_out.dtype))
     place = pltpu.HBM if fetching else pltpu.VMEM
     return pl.pallas_call(
-        lambda *refs: output_kernel(cuts, cols, fetching, *refs),
-        in_specs=[whole] * 2 + [pl.BlockSpec(memory_space=pl.ANY) if fetching else whole],
+        lambda *refs: output_kernel(cuts, cols, block, first_block, fetching, *refs),
+        in_specs=[whole, pl.BlockSpec(memory_space=pltpu.SMEM), whole]
+        + [pl.BlockSpec(memory_space=pl.ANY) if fetching else whole],
         out_specs=[whole] * len(out_shape),
         out_shape=out_shape,
-        scratch_shapes=[pltpu.SemaphoreType.DMA((model // cols,))] if fetching else [],
+        scratch_shapes=([pltpu.SemaphoreType.DMA((model // cols,))] if fetching else [])
+        + [pltpu.VMEM(returned.shape, jnp.bfloat16)],
         compiler_params=pltpu.CompilerParams(vmem_limit_bytes=12 * MIB),
-    )(slots_local, returned, pltpu.with_memory_space_constraint(w_out, place))
+    )(slots, devices, returned, pltpu.with_memory_space_constraint(w_out, place))
 
 
 def add_up_kernel(starts, extra, block, *refs):
@@ -357,27 +392,13 @@
         at = (place + way * steps + 2 * size) % size
         return owner * size + jnp.where(at < half, 2 * at, 2 * (size - 1 - at) + 1)
 
-    slot_blocks = slot_of.reshape(devices, block)
-
-    def slots_in(order):
-        pick = jnp.stack(order)[:, None] == jnp.arange(devices, dtype=jnp.int32)[None, :]
-        return jnp.sum(jnp.where(pick[:, :, None], slot_blocks[None], 0), axis=1).reshape(-1)
-
-    normed = norm(rows, norm_gain)
-    a, b = normed, swap(normed)
-    blocks, order = [a, b], [device_at(0, pool), device_at(0, 1 - pool)]
-    late, late_order = [], []
+    order = [device_at(0, pool), device_at(0, 1 - pool)]
+    late_order = []
     for k in range(1, half):
-        a, b = forward(a), forward(b)
-        blocks += [a, swap(a)]
         order += [device_at(-k, pool), device_at(k, 1 - pool)]
-        into, into_order = (blocks, order) if k < half - 1 else (late, late_order)
-        into += [b, swap(b)]
-        into_order += [device_at(-k, 1 - pool), device_at(k, pool)]
-    a = forward(a)
-    late += [a, swap(a)]
+        into = order if k < half - 1 else late_order
+        into += [device_at(-k, 1 - pool), device_at(k, pool)]
     late_order += [device_at(-half, pool), device_at(half, 1 - pool)]
-
     own_slots = lax.axis_index(AXES) * slots_dev + jnp.arange(slots_dev, dtype=jnp.int32)
     slot_len = jnp.sum(
         jnp.where(slot_of[None, :] == own_slots[:, None], lengths[None, :], 0), axis=1
@@ -394,22 +415,25 @@
     )
     rank = jnp.sum(shorter.astype(jnp.int32), axis=1)
     by_length = jnp.sum(jnp.where(rank[None, :] == each[:, None], each[None, :], 0), axis=1)
-    w_query, w_keyval, slot_len, by_length, slots_local, slots_early, slots_rest = (
-        lax.optimization_barrier(
-            (
-                w_query,
-                w_keyval,
-                slot_len,
-                by_length,
-                slots_in(order + late_order).reshape(1, -1),
-                slots_in(theirs + mine[:3]).reshape(1, -1),
-                slots_in(mine[3:]).reshape(1, -1),
-            )
-        )
-    )
+    owners = jnp.stack(order + late_order + theirs + mine)
+    index = (slot_len, by_length, owners, slot_of.reshape(1, -1))
+
+    normed = norm(rows, norm_gain)
+    a, b = normed, swap(normed)
+    b, index = lax.optimization_barrier((b, index))
+    slot_len, by_length, owners, slot_row = index
+    blocks, late = [a, b], []
+    for k in range(1, half):
+        a, b = forward(a), forward(b)
+        blocks += [a, swap(a)]
+        into = blocks if k < half - 1 else late
+        into += [b, swap(b)]
+    a = forward(a)
+    late += [a, swap(a)]
+
     depth = w_query.shape[0] // 8
     early_rows, *weights = project(blocks, (w_query, w_keyval), depth)
-    (sending,) = project(late, weights, depth, slots_local, early_rows)
+    (sending,) = project(late, weights, depth, slot_row, owners, early_rows)
     arrived = lax.all_to_all(sending, AXES, split_axis=0, concat_axis=0, tiled=True)
 
     attended = attend(by_length, slot_len, arrived, key_cache, value_cache, query_cols)
@@ -418,10 +442,11 @@
     rest = block * len(mine) - early
     cols = w_out.shape[1] // 8
     first, later, own_first, held = output(
-        (early, rest, early), slots_early, returned, w_out, cols, True
+        (early, rest, early), block, devices, slot_row, owners, returned, w_out, cols, True
     )
     first, later = swap(first), swap(later)
-    (own_later,) = output((rest,), slots_rest, returned, held, cols, False)
+    begun = devices + (2 * early + rest) // block
+    (own_later,) = output((rest,), block, begun, slot_row, owners, returned, held, cols, False)
 
     def chip_sum(items, arrivals=()):
         pieces = [(own_first, first, i) if i < 3 else (own_later, later, i - 3) for i in items]

time: 113 us -> 110 us (0.973)
  waiting for transfers between devices: 34.1 us -> 32 us
  Pallas kernels: 22.4 us -> 24.3 us
  local copies, waits for them, and re-layouts: 1.25 us -> 0.11 us
    ppermute x14, waiting for transfers between devices: 30.5 us -> 28.3 us  [body(): forward = lambda x: lax.ppermute(x, AXES, ring_pairs(size))]
    pallas_call x2, Pallas kernels: 5.99 us -> 7.68 us  [output(): pl.pallas_call(lambda *refs: output_kernel(cuts, cols, block, first_block...]
    ppermute x14, starting transfers between devices: 19.8 us -> 18.3 us  [body(): forward = lambda x: lax.ppermute(x, AXES, ring_pairs(size))]
  transfers between devices with their start and end apart: 25 -> 25, of which waited for: 15 -> 15; matrix products, arithmetic and copies ran while one was open for 3% -> 1% of each run, Pallas kernels for 8% -> 8%
where the time goes in v1:
time: 110 us
  waiting for transfers between devices  32 us (29%)
  blocking collectives  31.3 us (28%)
  Pallas kernels  24.3 us (22%)
  starting transfers between devices  20.5 us (19%)
  other arithmetic  1.18 us (1%)
    ppermute x14, waiting for transfers between devices, body(): forward = lambda x: lax.ppermute(x, AXES, ring_pairs(size))  28.3 us
    ppermute x14, starting transfers between devices, body(): forward = lambda x: lax.ppermute(x, AXES, ring_pairs(size))  18.3 us
    all_to_all x1, blocking collectives, body(): lax.all_to_all(sending, AXES, split_axis=0, concat_axis=0, tiled=True)  18 us
    all_to_all x1, blocking collectives, body(): lax.all_to_all(attended, AXES, split_axis=0, concat_axis=0, tiled=True)  13.4 us
    pallas_call x2, Pallas kernels, project(): pl.pallas_call(lambda *refs: project_kernel(count, last, depth, *refs), i...  8.18 us
    pallas_call x2, Pallas kernels, output(): pl.pallas_call(lambda *refs: output_kernel(cuts, cols, block, first_block...  7.68 us
    pallas_call x1, Pallas kernels, attend(): pl.pallas_call(lambda *refs: attend_kernel(query_cols, group, *refs), in_...  5.82 us
    ppermute x11, waiting for transfers between devices, body(): swap = lambda x: lax.ppermute(x, AXES, sibling_pairs(size))  3.68 us
  transfers between devices with their start and end apart: 25, of which 15 were waited for; matrix products, arithmetic and copies ran while one was open for 1% of the time, Pallas kernels for 8%

profile of v1, /device:TPU:0, one launch (start us, length us, event | category | flops | bytes accessed | tf_op | source)
XLA Modules:
  0.0 109.8 jit_solution(107007970631441177)
XLA Ops:
  0.0 1.2 %norm.1.refs_0_ = bf16[16,8192]{1,0:T(8,128)(2,1)S(1)} custom-call(bf16[16,8192]{1,0:T(8,128)(2,1)} %rows_ref.1, f32[1,8192]{1,0:T(1,128)} %bitcast.32), custom_call_target="tpu_custom_call" | custom-call | tf_op jit(solution)/shard_map/norm/pallas_call | solution.py:45
  1.2 0.6 collective-permute-start
  1.8 2.6 %collective-permute-start.5 = (bf16[16,8192]{1,0:T(8,128)(2,1)S(1)}, bf16[16,8192]{1,0:T(8,128)(2,1)S(1)}, u32[]{:S(2)}, u32[]{:S(2)}) collective-permute-start(bf16[16,8192]{1,0:T(8,128)(2,1)S(1)} %norm.1.refs_0_), channel_id=1, source_target_pairs={{0,2},{2,4},{4,6},{6,7},{7,5},{5,3},{3,1},{1,0},{8,9},{10,8},{12,1... | collective-permute-start | bytes 786440 | tf_op jit(solution)/shard_map/ppermute | solution.py:383
  4.4 0.9 select_reduce_fusion.refs_1_
  5.5 0.1 stack.89.refs_7_.refs_1_
  5.6 0.2 convert_reduce_fusion
  5.8 0.1 select_reduce_fusion.1.refs_0_
  5.9 1.6 %collective-permute-start.1 = (bf16[16,8192]{1,0:T(8,128)(2,1)S(1)}, bf16[16,8192]{1,0:T(8,128)(2,1)S(1)}, u32[]{:S(2)}, u32[]{:S(2)}) collective-permute-start(bf16[16,8192]{1,0:T(8,128)(2,1)S(1)} %collective-permute-done.refs_1_), channel_id=1, source_target_pairs={{0,2},{2,4},{4,6},{6,7},{7,5},{5,3},{3,1},{1,0},{8,9},{10,8},{12,1... | collective-permute-start | bytes 786440 | tf_op jit(solution)/shard_map/ppermute | solution.py:383
  7.5 1.1 %collective-permute-done.5.refs_2_ = bf16[16,8192]{1,0:T(8,128)(2,1)S(1)} collective-permute-done((bf16[16,8192]{1,0:T(8,128)(2,1)S(1)}, bf16[16,8192]{1,0:T(8,128)(2,1)S(1)}, u32[]{:S(2)}, u32[]{:S(2)}) %collective-permute-start.5) | collective-permute-done | bytes 262176 | tf_op jit(solution)/shard_map/ppermute | solution.py:383
  8.7 2.1 %collective-permute-start.6 = (bf16[16,8192]{1,0:T(8,128)(2,1)S(1)}, bf16[16,8192]{1,0:T(8,128)(2,1)S(1)}, u32[]{:S(2)}, u32[]{:S(2)}) collective-permute-start(bf16[16,8192]{1,0:T(8,128)(2,1)S(1)} %collective-permute-done.5.refs_2_), channel_id=1, source_target_pairs={{0,2},{2,4},{4,6},{6,7},{7,5},{5,3},{3,1},{1,0},{8,9},{10,8},{12,1... | collective-permute-start | bytes 786440 | tf_op jit(solution)/shard_map/ppermute | solution.py:383
  10.8 1.6 %collective-permute-done.1.refs_4_ = bf16[16,8192]{1,0:T(8,128)(2,1)S(1)} collective-permute-done((bf16[16,8192]{1,0:T(8,128)(2,1)S(1)}, bf16[16,8192]{1,0:T(8,128)(2,1)S(1)}, u32[]{:S(2)}, u32[]{:S(2)}) %collective-permute-start.1) | collective-permute-done | bytes 262176 | tf_op jit(solution)/shard_map/ppermute | solution.py:383
  12.3 1.6 %collective-permute-start.2 = (bf16[16,8192]{1,0:T(8,128)(2,1)S(1)}, bf16[16,8192]{1,0:T(8,128)(2,1)S(1)}, u32[]{:S(2)}, u32[]{:S(2)}) collective-permute-start(bf16[16,8192]{1,0:T(8,128)(2,1)S(1)} %collective-permute-done.1.refs_4_), channel_id=1, source_target_pairs={{0,2},{2,4},{4,6},{6,7},{7,5},{5,3},{3,1},{1,0},{8,9},{10,8},{12,1... | collective-permute-start | bytes 786440 | tf_op jit(solution)/shard_map/ppermute | solution.py:383
  13.9 1.2 %collective-permute-done.6.refs_6_ = bf16[16,8192]{1,0:T(8,128)(2,1)S(1)} collective-permute-done((bf16[16,8192]{1,0:T(8,128)(2,1)S(1)}, bf16[16,8192]{1,0:T(8,128)(2,1)S(1)}, u32[]{:S(2)}, u32[]{:S(2)}) %collective-permute-start.6) | collective-permute-done | bytes 262176 | tf_op jit(solution)/shard_map/ppermute | solution.py:383
  15.2 2.0 %collective-permute-start.7 = (bf16[16,8192]{1,0:T(8,128)(2,1)S(1)}, bf16[16,8192]{1,0:T(8,128)(2,1)S(1)}, u32[]{:S(2)}, u32[]{:S(2)}) collective-permute-start(bf16[16,8192]{1,0:T(8,128)(2,1)S(1)} %collective-permute-done.6.refs_6_), channel_id=1, source_target_pairs={{0,2},{2,4},{4,6},{6,7},{7,5},{5,3},{3,1},{1,0},{8,9},{10,8},{12,1... | collective-permute-start | bytes 786440 | tf_op jit(solution)/shard_map/ppermute | solution.py:383
  17.1 0.5 collective-permute-start.11
  17.6 1.1 collective-permute-done.2.refs_8_
  18.7 1.6 %collective-permute-start.3 = (bf16[16,8192]{1,0:T(8,128)(2,1)S(1)}, bf16[16,8192]{1,0:T(8,128)(2,1)S(1)}, u32[]{:S(2)}, u32[]{:S(2)}) collective-permute-start(bf16[16,8192]{1,0:T(8,128)(2,1)S(1)} %collective-permute-done.2.refs_8_), channel_id=1, source_target_pairs={{0,2},{2,4},{4,6},{6,7},{7,5},{5,3},{3,1},{1,0},{8,9},{10,8},{12,1... | collective-permute-start | bytes 786440 | tf_op jit(solution)/shard_map/ppermute | solution.py:383
  20.3 1.2 %collective-permute-done.7.refs_10_ = bf16[16,8192]{1,0:T(8,128)(2,1)S(1)} collective-permute-done((bf16[16,8192]{1,0:T(8,128)(2,1)S(1)}, bf16[16,8192]{1,0:T(8,128)(2,1)S(1)}, u32[]{:S(2)}, u32[]{:S(2)}) %collective-permute-start.7) | collective-permute-done | bytes 262176 | tf_op jit(solution)/shard_map/ppermute | solution.py:383
  21.5 2.0 %collective-permute-start.8 = (bf16[16,8192]{1,0:T(8,128)(2,1)S(1)}, bf16[16,8192]{1,0:T(8,128)(2,1)S(1)}, u32[]{:S(2)}, u32[]{:S(2)}) collective-permute-start(bf16[16,8192]{1,0:T(8,128)(2,1)S(1)} %collective-permute-done.7.refs_10_), channel_id=1, source_target_pairs={{0,2},{2,4},{4,6},{6,7},{7,5},{5,3},{3,1},{1,0},{8,9},{10,8},{12,1... | collective-permute-start | bytes 786440 | tf_op jit(solution)/shard_map/ppermute | solution.py:383
  23.5 0.5 collective-permute-start.13
  24.1 1.0 collective-permute-done.3.refs_0_
  25.1 2.8 %collective-permute-done.8.refs_2_ = bf16[16,8192]{1,0:T(8,128)(2,1)S(1)} collective-permute-done((bf16[16,8192]{1,0:T(8,128)(2,1)S(1)}, bf16[16,8192]{1,0:T(8,128)(2,1)S(1)}, u32[]{:S(2)}, u32[]{:S(2)}) %collective-permute-start.8) | collective-permute-done | bytes 262176 | tf_op jit(solution)/shard_map/ppermute | solution.py:383
  27.9 5.5 %shard_map.91 = (bf16[192,640]{1,0:T(8,128)(2,1)S(1)}, bf16[8192,512]{1,0:T(8,128)(2,1)S(1)}, bf16[8192,128]{1,0:T(8,128)(2,1)S(1)}) custom-call(bf16[16,8192]{1,0:T(8,128)(2,1)S(1)} %norm.1.refs_0_, bf16[16,8192]{1,0:T(8,128)(2,1)S(1)} %collective-permute-done.refs_1_, bf16[16,8192]{1,0:T(8,128)(2,1)S(1)} %collective-permute-done.5.refs_2_, ...), custom_call_target="tpu_custom_call" | custom-call | tf_op jit(solution)/shard_map/pallas_call | solution.py:132
  33.4 2.7 %shard_map.92 = bf16[256,640]{1,0:T(8,128)(2,1)S(1)} custom-call(bf16[16,8192]{1,0:T(8,128)(2,1)S(1)} %collective-permute-done.3.refs_0_, bf16[16,8192]{1,0:T(8,128)(2,1)S(1)} %collective-permute-done.4.refs_1_, bf16[16,8192]{1,0:T(8,128)(2,1)S(1)} %collective-permute-done.8.refs_2_, bf16[16,8192]{1,0:T(8,128)(2,1)S(1)} %collective-permute-done.9.refs_3_, ...), custom_call_target="tpu_custom_call" | custom-call | tf_op jit(solution)/shard_map/pallas_call | solution.py:132
  36.1 18.0 %all_to_all.22 = bf16[16,16,640]{2,1,0:T(8,128)(2,1)S(1)} all-to-all(bf16[16,16,640]{2,1,0:T(8,128)(2,1)S(1)} %bitcast.26), channel_id=1, replica_groups=mesh['groups'=2,'pool'=2,'tensor'=8] {'pool','tensor'}, dimensions={0} | all-to-all | bytes 655360 | tf_op jit(solution)/shard_map/all_to_all | solution.py:437
  54.1 5.8 %attend.1 = bf16[256,512]{1,0:T(8,128)(2,1)S(1)} custom-call(s32[16]{0:T(128)S(1)} %select_reduce_fusion.1.refs_0_, s32[16]{0:T(128)S(1)} %select_reduce_fusion.refs_1_, bf16[256,640]{1,0:T(8,128)(2,1)S(1)} %bitcast.27, bf16[16,256,1024]{2,1,0:T(8,128)(2,1)} %refs_3_.2, bf16[16,256,1024]{2,1,0:T(8,128)(2,1)} %refs_4_.1), custom_call_target="tpu_custom_call" | custom-call | tf_op jit(solution)/shard_map/attend/pallas_call | solution.py:269
  59.9 13.4 %all_to_all.23 = bf16[16,16,512]{2,1,0:T(8,128)(2,1)S(1)} all-to-all(bf16[16,16,512]{2,1,0:T(8,128)(2,1)S(1)} %bitcast.28), channel_id=1, replica_groups=mesh['groups'=2,'pool'=2,'tensor'=8] {'pool','tensor'}, dimensions={0} | all-to-all | bytes 524288 | tf_op jit(solution)/shard_map/all_to_all | solution.py:440
  73.3 5.3 %shard_map.93 = (bf16[48,8192]{1,0:T(8,128)(2,1)S(1)}, bf16[80,8192]{1,0:T(8,128)(2,1)S(1)}, bf16[48,8192]{1,0:T(8,128)(2,1)S(1)}, bf16[512,8192]{1,0:T(8,128)(2,1)S(1)}) custom-call(s32[1,256]{1,0:T(1,128)S(1)} %bitcast.30, s32[32]{0:T(128)S(1)} %stack.89.refs_7_.refs_1_, bf16[256,512]{1,0:T(8,128)(2,1)S(1)} %bitcast.24, bf16[512,8192]{1,0:T(8,128)(2,1)} %refs_3_.3), custom_call_target="tpu_custom_call" | custom-call | tf_op jit(solution)/shard_map/pallas_call | solution.py:339
  78.7 0.5 collective-permute-start.16
  79.2 3.6 %collective-permute-done.16.refs_1_.refs_3_ = bf16[48,8192]{1,0:T(8,128)(2,1)S(1)} collective-permute-done((bf16[48,8192]{1,0:T(8,128)(2,1)S(1)}, bf16[48,8192]{1,0:T(8,128)(2,1)S(1)}, u32[]{:S(2)}, u32[]{:S(2)}) %collective-permute-start.16) | collective-permute-done | bytes 786464 | tf_op jit(solution)/shard_map/ppermute | solution.py:384
  82.9 0.1 shard_map.95
  83.0 0.8 collective-permute-start.17
  83.9 2.3 %shard_map.94.refs_0_ = bf16[80,8192]{1,0:T(8,128)(2,1)S(1)} custom-call(s32[1,256]{1,0:T(1,128)S(1)} %bitcast.31, s32[32]{0:T(128)S(1)} %stack.89.refs_7_.refs_1_, bf16[256,512]{1,0:T(8,128)(2,1)S(1)} %bitcast.25, bf16[512,8192]{1,0:T(8,128)(2,1)S(1)} %get-tuple-element.27.refs_3_), custom_call_target="tpu_custom_call" | custom-call | tf_op jit(solution)/shard_map/pallas_call | solution.py:339
  86.2 3.2 %collective-permute-done.17.refs_2_ = bf16[16,8192]{1,0:T(8,128)(2,1)S(1)} collective-permute-done((bf16[16,8192]{1,0:T(8,128)(2,1)S(1)}, bf16[16,8192]{1,0:T(8,128)(2,1)S(1)}, u32[]{:S(2)}, u32[]{:S(2)}) %collective-permute-start.17) | collective-permute-done | bytes 262176 | tf_op jit(solution)/shard_map/ppermute | solution.py:383
  89.5 0.8 collective-permute-start.18
  90.3 1.9 %collective-permute-done.21.refs_2_ = bf16[16,8192]{1,0:T(8,128)(2,1)S(1)} collective-permute-done((bf16[16,8192]{1,0:T(8,128)(2,1)S(1)}, bf16[16,8192]{1,0:T(8,128)(2,1)S(1)}, u32[]{:S(2)}, u32[]{:S(2)}) %collective-permute-start.21) | collective-permute-done | bytes 262176 | tf_op jit(solution)/shard_map/ppermute | solution.py:383
  92.3 0.8 collective-permute-start.22
  93.1 2.8 %collective-permute-done.18.refs_2_ = bf16[16,8192]{1,0:T(8,128)(2,1)S(1)} collective-permute-done((bf16[16,8192]{1,0:T(8,128)(2,1)S(1)}, bf16[16,8192]{1,0:T(8,128)(2,1)S(1)}, u32[]{:S(2)}, u32[]{:S(2)}) %collective-permute-start.18) | collective-permute-done | bytes 262176 | tf_op jit(solution)/shard_map/ppermute | solution.py:383
  96.0 0.1 shard_map.97
  96.1 0.8 collective-permute-start.19
  96.8 1.9 %collective-permute-done.22.refs_2_ = bf16[16,8192]{1,0:T(8,128)(2,1)S(1)} collective-permute-done((bf16[16,8192]{1,0:T(8,128)(2,1)S(1)}, bf16[16,8192]{1,0:T(8,128)(2,1)S(1)}, u32[]{:S(2)}, u32[]{:S(2)}) %collective-permute-start.22) | collective-permute-done | bytes 262176 | tf_op jit(solution)/shard_map/ppermute | solution.py:383
  98.9 0.8 collective-permute-start.23
  99.7 2.8 %collective-permute-done.19.refs_2_ = bf16[16,8192]{1,0:T(8,128)(2,1)S(1)} collective-permute-done((bf16[16,8192]{1,0:T(8,128)(2,1)S(1)}, bf16[16,8192]{1,0:T(8,128)(2,1)S(1)}, u32[]{:S(2)}, u32[]{:S(2)}) %collective-permute-start.19) | collective-permute-done | bytes 262176 | tf_op jit(solution)/shard_map/ppermute | solution.py:383
  102.5 0.1 shard_map.98
  102.6 0.8 collective-permute-start.20
  103.4 1.9 %collective-permute-done.23 = bf16[16,8192]{1,0:T(8,128)(2,1)S(1)} collective-permute-done((bf16[16,8192]{1,0:T(8,128)(2,1)S(1)}, bf16[16,8192]{1,0:T(8,128)(2,1)S(1)}, u32[]{:S(2)}, u32[]{:S(2)}) %collective-permute-start.23) | collective-permute-done | bytes 262176 | tf_op jit(solution)/shard_map/ppermute | solution.py:383
  105.3 3.7 %collective-permute-done.20.refs_2_ = bf16[16,8192]{1,0:T(8,128)(2,1)S(1)} collective-permute-done((bf16[16,8192]{1,0:T(8,128)(2,1)S(1)}, bf16[16,8192]{1,0:T(8,128)(2,1)S(1)}, u32[]{:S(2)}, u32[]{:S(2)}) %collective-permute-start.20) | collective-permute-done | bytes 262176 | tf_op jit(solution)/shard_map/ppermute | solution.py:383
  109.0 0.8 shard_map.101
  (24 shorter events, 0.5 us)
Async XLA Ops:
  0.0 33.4 %copy-start = (s32[256]{0:T(256)S(1)}, s32[256]{0:T(256)}, u32[]{:S(2)}) copy-start(s32[256]{0:T(256)} %param.17) | copy-start | bytes 3076
  1.2 4.7 %collective-permute-start = (bf16[16,8192]{1,0:T(8,128)(2,1)S(1)}, bf16[16,8192]{1,0:T(8,128)(2,1)S(1)}, u32[]{:S(2)}, u32[]{:S(2)}) collective-permute-start(bf16[16,8192]{1,0:T(8,128)(2,1)S(1)} %norm.1.refs_0_), channel_id=1, source_target_pairs={{0,8},{1,9},{2,10},{3,11},{4,12},{5,13},{6,14},{7,15},{8,0},{9,1},... | collective-permute-start | bytes 786440 | tf_op jit(solution)/shard_map/ppermute | solution.py:384
  1.8 6.9 %collective-permute-start.5 = (bf16[16,8192]{1,0:T(8,128)(2,1)S(1)}, bf16[16,8192]{1,0:T(8,128)(2,1)S(1)}, u32[]{:S(2)}, u32[]{:S(2)}) collective-permute-start(bf16[16,8192]{1,0:T(8,128)(2,1)S(1)} %norm.1.refs_0_), channel_id=1, source_target_pairs={{0,2},{2,4},{4,6},{6,7},{7,5},{5,3},{3,1},{1,0},{8,9},{10,8},{12,1... | collective-permute-start | bytes 786440 | tf_op jit(solution)/shard_map/ppermute | solution.py:383
  5.9 6.4 %collective-permute-start.1 = (bf16[16,8192]{1,0:T(8,128)(2,1)S(1)}, bf16[16,8192]{1,0:T(8,128)(2,1)S(1)}, u32[]{:S(2)}, u32[]{:S(2)}) collective-permute-start(bf16[16,8192]{1,0:T(8,128)(2,1)S(1)} %collective-permute-done.refs_1_), channel_id=1, source_target_pairs={{0,2},{2,4},{4,6},{6,7},{7,5},{5,3},{3,1},{1,0},{8,9},{10,8},{12,1... | collective-permute-start | bytes 786440 | tf_op jit(solution)/shard_map/ppermute | solution.py:383
  8.7 6.5 %collective-permute-start.6 = (bf16[16,8192]{1,0:T(8,128)(2,1)S(1)}, bf16[16,8192]{1,0:T(8,128)(2,1)S(1)}, u32[]{:S(2)}, u32[]{:S(2)}) collective-permute-start(bf16[16,8192]{1,0:T(8,128)(2,1)S(1)} %collective-permute-done.5.refs_2_), channel_id=1, source_target_pairs={{0,2},{2,4},{4,6},{6,7},{7,5},{5,3},{3,1},{1,0},{8,9},{10,8},{12,1... | collective-permute-start | bytes 786440 | tf_op jit(solution)/shard_map/ppermute | solution.py:383
  12.3 6.4 %collective-permute-start.2 = (bf16[16,8192]{1,0:T(8,128)(2,1)S(1)}, bf16[16,8192]{1,0:T(8,128)(2,1)S(1)}, u32[]{:S(2)}, u32[]{:S(2)}) collective-permute-start(bf16[16,8192]{1,0:T(8,128)(2,1)S(1)} %collective-permute-done.1.refs_4_), channel_id=1, source_target_pairs={{0,2},{2,4},{4,6},{6,7},{7,5},{5,3},{3,1},{1,0},{8,9},{10,8},{12,1... | collective-permute-start | bytes 786440 | tf_op jit(solution)/shard_map/ppermute | solution.py:383
  15.2 6.4 %collective-permute-start.7 = (bf16[16,8192]{1,0:T(8,128)(2,1)S(1)}, bf16[16,8192]{1,0:T(8,128)(2,1)S(1)}, u32[]{:S(2)}, u32[]{:S(2)}) collective-permute-start(bf16[16,8192]{1,0:T(8,128)(2,1)S(1)} %collective-permute-done.6.refs_6_), channel_id=1, source_target_pairs={{0,2},{2,4},{4,6},{6,7},{7,5},{5,3},{3,1},{1,0},{8,9},{10,8},{12,1... | collective-permute-start | bytes 786440 | tf_op jit(solution)/shard_map/ppermute | solution.py:383
  17.1 6.4 %collective-permute-start.10 = (bf16[16,8192]{1,0:T(8,128)(2,1)S(1)}, bf16[16,8192]{1,0:T(8,128)(2,1)S(1)}, u32[]{:S(2)}, u32[]{:S(2)}) collective-permute-start(bf16[16,8192]{1,0:T(8,128)(2,1)S(1)} %collective-permute-done.5.refs_2_), channel_id=1, source_target_pairs={{0,8},{1,9},{2,10},{3,11},{4,12},{5,13},{6,14},{7,15},{8,0},{9,1},... | collective-permute-start | bytes 786440 | tf_op jit(solution)/shard_map/ppermute | solution.py:384
  17.1 6.9 %collective-permute-start.11 = (bf16[16,8192]{1,0:T(8,128)(2,1)S(1)}, bf16[16,8192]{1,0:T(8,128)(2,1)S(1)}, u32[]{:S(2)}, u32[]{:S(2)}) collective-permute-start(bf16[16,8192]{1,0:T(8,128)(2,1)S(1)} %collective-permute-done.1.refs_4_), channel_id=1, source_target_pairs={{0,8},{1,9},{2,10},{3,11},{4,12},{5,13},{6,14},{7,15},{8,0},{9,1},... | collective-permute-start | bytes 786440 | tf_op jit(solution)/shard_map/ppermute | solution.py:384
  18.7 6.4 %collective-permute-start.3 = (bf16[16,8192]{1,0:T(8,128)(2,1)S(1)}, bf16[16,8192]{1,0:T(8,128)(2,1)S(1)}, u32[]{:S(2)}, u32[]{:S(2)}) collective-permute-start(bf16[16,8192]{1,0:T(8,128)(2,1)S(1)} %collective-permute-done.2.refs_8_), channel_id=1, source_target_pairs={{0,2},{2,4},{4,6},{6,7},{7,5},{5,3},{3,1},{1,0},{8,9},{10,8},{12,1... | collective-permute-start | bytes 786440 | tf_op jit(solution)/shard_map/ppermute | solution.py:383
  21.5 6.4 %collective-permute-start.8 = (bf16[16,8192]{1,0:T(8,128)(2,1)S(1)}, bf16[16,8192]{1,0:T(8,128)(2,1)S(1)}, u32[]{:S(2)}, u32[]{:S(2)}) collective-permute-start(bf16[16,8192]{1,0:T(8,128)(2,1)S(1)} %collective-permute-done.7.refs_10_), channel_id=1, source_target_pairs={{0,2},{2,4},{4,6},{6,7},{7,5},{5,3},{3,1},{1,0},{8,9},{10,8},{12,1... | collective-permute-start | bytes 786440 | tf_op jit(solution)/shard_map/ppermute | solution.py:383
  23.5 4.4 %collective-permute-start.12 = (bf16[16,8192]{1,0:T(8,128)(2,1)S(1)}, bf16[16,8192]{1,0:T(8,128)(2,1)S(1)}, u32[]{:S(2)}, u32[]{:S(2)}) collective-permute-start(bf16[16,8192]{1,0:T(8,128)(2,1)S(1)} %collective-permute-done.6.refs_6_), channel_id=1, source_target_pairs={{0,8},{1,9},{2,10},{3,11},{4,12},{5,13},{6,14},{7,15},{8,0},{9,1},... | collective-permute-start | bytes 786440 | tf_op jit(solution)/shard_map/ppermute | solution.py:384
  23.5 4.4 %collective-permute-start.13 = (bf16[16,8192]{1,0:T(8,128)(2,1)S(1)}, bf16[16,8192]{1,0:T(8,128)(2,1)S(1)}, u32[]{:S(2)}, u32[]{:S(2)}) collective-permute-start(bf16[16,8192]{1,0:T(8,128)(2,1)S(1)} %collective-permute-done.2.refs_8_), channel_id=1, source_target_pairs={{0,8},{1,9},{2,10},{3,11},{4,12},{5,13},{6,14},{7,15},{8,0},{9,1},... | collective-permute-start | bytes 786440 | tf_op jit(solution)/shard_map/ppermute | solution.py:384
  24.0 3.9 %collective-permute-start.14 = (bf16[16,8192]{1,0:T(8,128)(2,1)S(1)}, bf16[16,8192]{1,0:T(8,128)(2,1)S(1)}, u32[]{:S(2)}, u32[]{:S(2)}) collective-permute-start(bf16[16,8192]{1,0:T(8,128)(2,1)S(1)} %collective-permute-done.7.refs_10_), channel_id=1, source_target_pairs={{0,8},{1,9},{2,10},{3,11},{4,12},{5,13},{6,14},{7,15},{8,0},{9,1},... | collective-permute-start | bytes 786440 | tf_op jit(solution)/shard_map/ppermute | solution.py:384
  25.1 8.3 %collective-permute-start.4 = (bf16[16,8192]{1,0:T(8,128)(2,1)S(1)}, bf16[16,8192]{1,0:T(8,128)(2,1)S(1)}, u32[]{:S(2)}, u32[]{:S(2)}) collective-permute-start(bf16[16,8192]{1,0:T(8,128)(2,1)S(1)} %collective-permute-done.3.refs_0_), channel_id=1, source_target_pairs={{0,8},{1,9},{2,10},{3,11},{4,12},{5,13},{6,14},{7,15},{8,0},{9,1},... | collective-permute-start | bytes 786440 | tf_op jit(solution)/shard_map/ppermute | solution.py:384
  27.9 5.5 %collective-permute-start.9 = (bf16[16,8192]{1,0:T(8,128)(2,1)S(1)}, bf16[16,8192]{1,0:T(8,128)(2,1)S(1)}, u32[]{:S(2)}, u32[]{:S(2)}) collective-permute-start(bf16[16,8192]{1,0:T(8,128)(2,1)S(1)} %collective-permute-done.8.refs_2_), channel_id=1, source_target_pairs={{0,8},{1,9},{2,10},{3,11},{4,12},{5,13},{6,14},{7,15},{8,0},{9,1},... | collective-permute-start | bytes 786440 | tf_op jit(solution)/shard_map/ppermute | solution.py:384
  78.7 13.6 %collective-permute-start.15 = (bf16[80,8192]{1,0:T(8,128)(2,1)S(1)}, bf16[80,8192]{1,0:T(8,128)(2,1)S(1)}, u32[]{:S(2)}, u32[]{:S(2)}) collective-permute-start(bf16[80,8192]{1,0:T(8,128)(2,1)S(1)} %get-tuple-element.28), channel_id=1, source_target_pairs={{0,8},{1,9},{2,10},{3,11},{4,12},{5,13},{6,14},{7,15},{8,0},{9,1},... | collective-permute-start | bytes 3932168 | tf_op jit(solution)/shard_map/ppermute | solution.py:384
  78.7 4.1 %collective-permute-start.16 = (bf16[48,8192]{1,0:T(8,128)(2,1)S(1)}, bf16[48,8192]{1,0:T(8,128)(2,1)S(1)}, u32[]{:S(2)}, u32[]{:S(2)}) collective-permute-start(bf16[48,8192]{1,0:T(8,128)(2,1)S(1)} %get-tuple-element.30), channel_id=1, source_target_pairs={{0,8},{1,9},{2,10},{3,11},{4,12},{5,13},{6,14},{7,15},{8,0},{9,1},... | collective-permute-start | bytes 2359304 | tf_op jit(solution)/shard_map/ppermute | solution.py:384
  83.0 6.4 %collective-permute-start.17 = (bf16[16,8192]{1,0:T(8,128)(2,1)S(1)}, bf16[16,8192]{1,0:T(8,128)(2,1)S(1)}, u32[]{:S(2)}, u32[]{:S(2)}) collective-permute-start(bf16[16,8192]{1,0:T(8,128)(2,1)S(1)} %get-tuple-element.31), channel_id=1, source_target_pairs={{0,2},{2,4},{4,6},{6,7},{7,5},{5,3},{3,1},{1,0},{8,9},{10,8},{12,1... | collective-permute-start | bytes 786440 | tf_op jit(solution)/shard_map/ppermute | solution.py:383
  83.8 8.4 %collective-permute-start.21 = (bf16[16,8192]{1,0:T(8,128)(2,1)S(1)}, bf16[16,8192]{1,0:T(8,128)(2,1)S(1)}, u32[]{:S(2)}, u32[]{:S(2)}) collective-permute-start(bf16[16,8192]{1,0:T(8,128)(2,1)S(1)} %get-tuple-element.32), channel_id=1, source_target_pairs={{0,2},{2,4},{4,6},{6,7},{7,5},{5,3},{3,1},{1,0},{8,9},{10,8},{12,1... | collective-permute-start | bytes 786440 | tf_op jit(solution)/shard_map/ppermute | solution.py:383
  89.5 6.4 %collective-permute-start.18 = (bf16[16,8192]{1,0:T(8,128)(2,1)S(1)}, bf16[16,8192]{1,0:T(8,128)(2,1)S(1)}, u32[]{:S(2)}, u32[]{:S(2)}) collective-permute-start(bf16[16,8192]{1,0:T(8,128)(2,1)S(1)} %shard_map.96), channel_id=1, source_target_pairs={{0,2},{2,4},{4,6},{6,7},{7,5},{5,3},{3,1},{1,0},{8,9},{10,8},{12,1... | collective-permute-start | bytes 786440 | tf_op jit(solution)/shard_map/ppermute | solution.py:383
  92.3 6.4 %collective-permute-start.22 = (bf16[16,8192]{1,0:T(8,128)(2,1)S(1)}, bf16[16,8192]{1,0:T(8,128)(2,1)S(1)}, u32[]{:S(2)}, u32[]{:S(2)}) collective-permute-start(bf16[16,8192]{1,0:T(8,128)(2,1)S(1)} %shard_map.99), channel_id=1, source_target_pairs={{0,2},{2,4},{4,6},{6,7},{7,5},{5,3},{3,1},{1,0},{8,9},{10,8},{12,1... | collective-permute-start | bytes 786440 | tf_op jit(solution)/shard_map/ppermute | solution.py:383
  96.1 6.4 %collective-permute-start.19 = (bf16[16,8192]{1,0:T(8,128)(2,1)S(1)}, bf16[16,8192]{1,0:T(8,128)(2,1)S(1)}, u32[]{:S(2)}, u32[]{:S(2)}) collective-permute-start(bf16[16,8192]{1,0:T(8,128)(2,1)S(1)} %shard_map.97), channel_id=1, source_target_pairs={{0,2},{2,4},{4,6},{6,7},{7,5},{5,3},{3,1},{1,0},{8,9},{10,8},{12,1... | collective-permute-start | bytes 786440 | tf_op jit(solution)/shard_map/ppermute | solution.py:383
  98.9 6.4 %collective-permute-start.23 = (bf16[16,8192]{1,0:T(8,128)(2,1)S(1)}, bf16[16,8192]{1,0:T(8,128)(2,1)S(1)}, u32[]{:S(2)}, u32[]{:S(2)}) collective-permute-start(bf16[16,8192]{1,0:T(8,128)(2,1)S(1)} %shard_map.100), channel_id=1, source_target_pairs={{0,2},{2,4},{4,6},{6,7},{7,5},{5,3},{3,1},{1,0},{8,9},{10,8},{12,1... | collective-permute-start | bytes 786440 | tf_op jit(solution)/shard_map/ppermute | solution.py:383
  102.6 6.4 %collective-permute-start.20 = (bf16[16,8192]{1,0:T(8,128)(2,1)S(1)}, bf16[16,8192]{1,0:T(8,128)(2,1)S(1)}, u32[]{:S(2)}, u32[]{:S(2)}) collective-permute-start(bf16[16,8192]{1,0:T(8,128)(2,1)S(1)} %shard_map.98), channel_id=1, source_target_pairs={{0,2},{2,4},{4,6},{6,7},{7,5},{5,3},{3,1},{1,0},{8,9},{10,8},{12,1... | collective-permute-start | bytes 786440 | tf_op jit(solution)/shard_map/ppermute | solution.py:383
  105.3 3.7 %collective-permute-start.24 = (bf16[16,8192]{1,0:T(8,128)(2,1)S(1)}, bf16[16,8192]{1,0:T(8,128)(2,1)S(1)}, u32[]{:S(2)}, u32[]{:S(2)}) collective-permute-start(bf16[16,8192]{1,0:T(8,128)(2,1)S(1)} %collective-permute-done.23), channel_id=1, source_target_pairs={{0,8},{1,9},{2,10},{3,11},{4,12},{5,13},{6,14},{7,15},{8,0},{9,1},... | collective-permute-start | bytes 786440 | tf_op jit(solution)/shard_map/ppermute | solution.py:384

commit v2 on v0

--- a/solution.py
+++ b/solution.py
@@ -14,6 +14,8 @@
 MIB = 1 << 20
 CHUNK = 64
 GROUP = 4
+PIECES = 4
+DEPTH = 1024
 
 
 def ring_order(size):
@@ -51,41 +53,57 @@
     )(*[pltpu.with_memory_space_constraint(x, pltpu.HBM) for x in (rows, gain.reshape(1, -1))])
 
 
-def project_kernel(count, last, depth, *refs):
+def fetch_kernel(count, start, *refs):
+    sems = refs[2 * count]
+    copies = [
+        pltpu.make_async_copy(
+            refs[i].at[pl.ds(start, refs[count + i].shape[0])], refs[count + i], sems.at[i]
+        )
+        for i in range(count)
+    ]
+    for copy in copies:
+        copy.start()
+    for copy in copies:
+        copy.wait()
+
+
+def fetch(start, rows, *arrays):
+    count = len(arrays)
+    size = sum(rows * x.shape[1] * x.dtype.itemsize for x in arrays)
+    return pl.pallas_call(
+        lambda *refs: fetch_kernel(count, start, *refs),
+        in_specs=[pl.BlockSpec(memory_space=pl.ANY)] * count,
+        out_specs=[pl.BlockSpec(memory_space=pltpu.VMEM)] * count,
+        out_shape=[pltpu.VMEM((rows, x.shape[1]), x.dtype) for x in arrays],
+        scratch_shapes=[pltpu.SemaphoreType.DMA((count,))],
+        compiler_params=pltpu.CompilerParams(vmem_limit_bytes=MIB),
+        cost_estimate=pl.CostEstimate(flops=0, bytes_accessed=2 * size, transcendentals=0),
+    )(*[pltpu.with_memory_space_constraint(x, pltpu.HBM) for x in arrays])
+
+
+def project_kernel(count, held, last, *refs):
     blocks = refs[:count]
-    wq_ref, wkv_ref = refs[count : count + 2]
-    starts = range(0, wq_ref.shape[0], depth)
+    pieces = [refs[count + 2 * i : count + 2 * i + 2] for i in range(held)]
     if last:
-        slots_ref, before_ref, out_ref, acc = refs[count + 2 :]
+        slots_ref, before_ref, out_ref, acc = refs[count + 2 * held :]
     else:
-        out_ref, wq_held, wkv_held, acc, sems = refs[count + 2 :]
-        copies = []
-        for i, start in enumerate(starts):
-            cut = pl.ds(start, depth)
-            copies.append(
-                [
-                    pltpu.make_async_copy(wq_ref.at[cut], wq_held.at[cut], sems.at[0, i]),
-                    pltpu.make_async_copy(wkv_ref.at[cut], wkv_held.at[cut], sems.at[1, i]),
-                ]
-            )
-            for copy in copies[-1]:
-                copy.start()
-        wq_ref, wkv_ref = wq_held, wkv_held
-    query_cols = wq_ref.shape[1]
-    for i, start in enumerate(starts):
-        cut = slice(start, start + depth)
-        part = jnp.concatenate([b[:, cut] for b in blocks], axis=0)
-        if not last:
-            for copy in copies[i]:
-                copy.wait()
-        query = jnp.dot(part, wq_ref[cut, :], preferred_element_type=jnp.float32)
-        keyval = jnp.dot(part, wkv_ref[cut, :], preferred_element_type=jnp.float32)
-        if i == 0:
-            acc[:, :query_cols] = query
-            acc[:, query_cols:] = keyval
-        else:
-            acc[:, :query_cols] += query
-            acc[:, query_cols:] += keyval
+        out_ref, acc = refs[count + 2 * held :]
+    query_cols = pieces[0][0].shape[1]
+    rows = pieces[0][0].shape[0]
+    depth = min(rows, DEPTH)
+    for i, (wq_ref, wkv_ref) in enumerate(pieces):
+        for start in range(0, rows, depth):
+            cut = slice(start, start + depth)
+            at = i * rows + start
+            part = jnp.concatenate([b[:, at : at + depth] for b in blocks], axis=0)
+            query = jnp.dot(part, wq_ref[cut, :], preferred_element_type=jnp.float32)
+            keyval = jnp.dot(part, wkv_ref[cut, :], preferred_element_type=jnp.float32)
+            if at == 0:
+                acc[:, :query_cols] = query
+                acc[:, query_cols:] = keyval
+            else:
+                acc[:, :query_cols] += query
+                acc[:, query_cols:] += keyval
     if not last:
         out_ref[...] = acc[...].astype(jnp.bfloat16)
         return
@@ -96,29 +114,22 @@
     out_ref[...] = jnp.dot(order, both, preferred_element_type=jnp.float32).astype(jnp.bfloat16)
 
 
-def project(blocks, weights, depth, slots=None, before=None):
+def project(blocks, pieces, slots=None, before=None):
     count = len(blocks)
     rows = sum(b.shape[0] for b in blocks)
-    width = sum(w.shape[1] for w in weights)
+    width = sum(w.shape[1] for w in pieces[0])
     last = slots is not None
     whole = pl.BlockSpec(memory_space=pltpu.VMEM)
-    place = pltpu.VMEM if last else pltpu.HBM
-    operands = list(blocks) + [pltpu.with_memory_space_constraint(w, place) for w in weights]
-    specs = [whole] * count + [whole if last else pl.BlockSpec(memory_space=pl.ANY)] * 2
-    out_shape = [jax.ShapeDtypeStruct((slots.shape[1] if last else rows, width), jnp.bfloat16)]
-    scratch = [pltpu.VMEM((rows, width), jnp.float32)]
-    if last:
-        operands += [slots, before]
-        specs += [whole] * 2
-    else:
-        out_shape += [pltpu.VMEM(w.shape, w.dtype) for w in weights]
-        scratch.append(pltpu.SemaphoreType.DMA((2, weights[0].shape[0] // depth)))
-    return pl.pallas_call(
-        lambda *refs: project_kernel(count, last, depth, *refs),
-        in_specs=specs,
-        out_specs=[whole] * len(out_shape),
-        out_shape=out_shape,
-        scratch_shapes=scratch,
+    operands = list(blocks)
+    operands += [pltpu.with_memory_space_constraint(w, pltpu.VMEM) for p in pieces for w in p]
+    operands += [slots, before] if last else []
+    out_rows = slots.shape[1] if last else rows
+    return pl.pallas_call(
+        lambda *refs: project_kernel(count, len(pieces), last, *refs),
+        in_specs=[whole] * len(operands),
+        out_specs=whole,
+        out_shape=jax.ShapeDtypeStruct((out_rows, width), jnp.bfloat16),
+        scratch_shapes=[pltpu.VMEM((rows, width), jnp.float32)],
         compiler_params=pltpu.CompilerParams(vmem_limit_bytes=16 * MIB),
     )(*operands)
 
@@ -363,21 +374,13 @@
         pick = jnp.stack(order)[:, None] == jnp.arange(devices, dtype=jnp.int32)[None, :]
         return jnp.sum(jnp.where(pick[:, :, None], slot_blocks[None], 0), axis=1).reshape(-1)
 
-    normed = norm(rows, norm_gain)
-    a, b = normed, swap(normed)
-    blocks, order = [a, b], [device_at(0, pool), device_at(0, 1 - pool)]
-    late, late_order = [], []
+    order = [device_at(0, pool), device_at(0, 1 - pool)]
+    late_order = []
     for k in range(1, half):
-        a, b = forward(a), forward(b)
-        blocks += [a, swap(a)]
         order += [device_at(-k, pool), device_at(k, 1 - pool)]
-        into, into_order = (blocks, order) if k < half - 1 else (late, late_order)
-        into += [b, swap(b)]
-        into_order += [device_at(-k, 1 - pool), device_at(k, pool)]
-    a = forward(a)
-    late += [a, swap(a)]
+        into = order if k < half - 1 else late_order
+        into += [device_at(-k, 1 - pool), device_at(k, pool)]
     late_order += [device_at(-half, pool), device_at(half, 1 - pool)]
-
     own_slots = lax.axis_index(AXES) * slots_dev + jnp.arange(slots_dev, dtype=jnp.int32)
     slot_len = jnp.sum(
         jnp.where(slot_of[None, :] == own_slots[:, None], lengths[None, :], 0), axis=1
@@ -394,22 +397,32 @@
     )
     rank = jnp.sum(shorter.astype(jnp.int32), axis=1)
     by_length = jnp.sum(jnp.where(rank[None, :] == each[:, None], each[None, :], 0), axis=1)
-    w_query, w_keyval, slot_len, by_length, slots_local, slots_early, slots_rest = (
-        lax.optimization_barrier(
-            (
-                w_query,
-                w_keyval,
-                slot_len,
-                by_length,
-                slots_in(order + late_order).reshape(1, -1),
-                slots_in(theirs + mine[:3]).reshape(1, -1),
-                slots_in(mine[3:]).reshape(1, -1),
-            )
-        )
-    )
-    depth = w_query.shape[0] // 8
-    early_rows, *weights = project(blocks, (w_query, w_keyval), depth)
-    (sending,) = project(late, weights, depth, slots_local, early_rows)
+    index = (
+        slot_len,
+        by_length,
+        slots_in(order + late_order).reshape(1, -1),
+        slots_in(theirs).reshape(1, -1),
+        slots_in(mine[:3]).reshape(1, -1),
+        slots_in(mine[3:]).reshape(1, -1),
+    )
+
+    normed = norm(rows, norm_gain)
+    a, b = normed, swap(normed)
+    b, index = lax.optimization_barrier((b, index))
+    slot_len, by_length, slots_local, slots_theirs, slots_early, slots_rest = index
+    blocks, late = [a, b], []
+    for k in range(1, half):
+        a, b = forward(a), forward(b)
+        blocks += [a, swap(a)]
+        into = blocks if k < half - 1 else late
+        into += [b, swap(b)]
+    a = forward(a)
+    late += [a, swap(a)]
+
+    part = w_query.shape[0] // PIECES
+    pieces = [fetch(i * part, part, w_query, w_keyval) for i in range(PIECES)]
+    early_rows = project(blocks, pieces)
+    sending = project(late, pieces, slots_local, early_rows)
     arrived = lax.all_to_all(sending, AXES, split_axis=0, concat_axis=0, tiled=True)
 
     attended = attend(by_length, slot_len, arrived, key_cache, value_cache, query_cols)
@@ -417,10 +430,9 @@
     early = 3 * block
     rest = block * len(mine) - early
     cols = w_out.shape[1] // 8
-    first, later, own_first, held = output(
-        (early, rest, early), slots_early, returned, w_out, cols, True
-    )
+    first, later, held = output((early, rest), slots_theirs, returned, w_out, cols, True)
     first, later = swap(first), swap(later)
+    (own_first,) = output((early,), slots_early, returned, held, cols, False)
     (own_later,) = output((rest,), slots_rest, returned, held, cols, False)
 
     def chip_sum(items, arrivals=()):

time: 113 us -> 112 us (level)
  Pallas kernels: 22.4 us -> 26.5 us
  starting transfers between devices: 21.6 us -> 19.2 us
  waiting for transfers between devices: 34.1 us -> 32.2 us
  blocking collectives: 31.8 us -> 30.3 us
    ppermute x14, starting transfers between devices: 19.8 us -> 17 us  [body(): forward = lambda x: lax.ppermute(x, AXES, ring_pairs(size))]
    pallas_call x2 -> x6, Pallas kernels: 8.63 us -> 11.5 us  [the longest x4 6.77 us: fetch(): pl.pallas_call(lambda *refs: fetch_kernel(count, start, *refs), in_specs=...]
    ppermute x11, waiting for transfers between devices: 3.68 us -> 1.94 us  [body(): swap = lambda x: lax.ppermute(x, AXES, sibling_pairs(size))]
    all_to_all x1, blocking collectives: 18 us -> 16.5 us  [body(): lax.all_to_all(sending, AXES, split_axis=0, concat_axis=0, tiled=True)]
    pallas_call x2 -> x3, Pallas kernels: 5.99 us -> 7.3 us  [output(): pl.pallas_call(lambda *refs: output_kernel(cuts, cols, fetching, *refs),...]
  transfers between devices with their start and end apart: 25 -> 25, of which waited for: 15 -> 14; matrix products, arithmetic and copies ran while one was open for 3% -> 3% of each run, Pallas kernels for 8% -> 12%
where the time goes in v2:
time: 112 us
  waiting for transfers between devices  32.2 us (29%)
  blocking collectives  30.3 us (27%)
  Pallas kernels  26.5 us (24%)
  starting transfers between devices  19.2 us (17%)
  other arithmetic  1.97 us (2%)
  local copies, waits for them, and re-layouts  1.34 us (1%)
    ppermute x14, waiting for transfers between devices, body(): forward = lambda x: lax.ppermute(x, AXES, ring_pairs(size))  30.3 us
    ppermute x14, starting transfers between devices, body(): forward = lambda x: lax.ppermute(x, AXES, ring_pairs(size))  17 us
    all_to_all x1, blocking collectives, body(): lax.all_to_all(sending, AXES, split_axis=0, concat_axis=0, tiled=True)  16.5 us
    all_to_all x1, blocking collectives, body(): lax.all_to_all(attended, AXES, split_axis=0, concat_axis=0, tiled=True)  13.7 us
    pallas_call x3, Pallas kernels, output(): pl.pallas_call(lambda *refs: output_kernel(cuts, cols, fetching, *refs),...  7.3 us
    pallas_call x4, Pallas kernels, fetch(): pl.pallas_call(lambda *refs: fetch_kernel(count, start, *refs), in_specs=...  6.77 us
    pallas_call x1, Pallas kernels, attend(): pl.pallas_call(lambda *refs: attend_kernel(query_cols, group, *refs), in_...  5.1 us
    pallas_call x2, Pallas kernels, project(): pl.pallas_call(lambda *refs: project_kernel(count, len(pieces), last, *re...  4.69 us
  transfers between devices with their start and end apart: 25, of which 14 were waited for; matrix products, arithmetic and copies ran while one was open for 3% of the time, Pallas kernels for 12%

profile of v2, /device:TPU:0, one launch (start us, length us, event | category | flops | bytes accessed | tf_op | source)
XLA Modules:
  0.0 111.7 jit_solution(7966228226726702198)
XLA Ops:
  0.0 1.2 %norm.1.refs_0_ = bf16[16,8192]{1,0:T(8,128)(2,1)S(1)} custom-call(bf16[16,8192]{1,0:T(8,128)(2,1)} %rows_ref.1, f32[1,8192]{1,0:T(1,128)} %bitcast.29), custom_call_target="tpu_custom_call" | custom-call | tf_op jit(solution)/shard_map/norm/pallas_call | solution.py:46
  1.2 0.6 collective-permute-start
  1.7 2.6 %collective-permute-start.5 = (bf16[16,8192]{1,0:T(8,128)(2,1)S(1)}, bf16[16,8192]{1,0:T(8,128)(2,1)S(1)}, u32[]{:S(2)}, u32[]{:S(2)}) collective-permute-start(bf16[16,8192]{1,0:T(8,128)(2,1)S(1)} %norm.1.refs_0_), channel_id=1, source_target_pairs={{0,2},{2,4},{4,6},{6,7},{7,5},{5,3},{3,1},{1,0},{8,9},{10,8},{12,1... | collective-permute-start | bytes 786440 | tf_op jit(solution)/shard_map/ppermute | solution.py:359
  4.5 0.8 broadcast_in_dim.132
  6.2 0.9 select_reduce_fusion.4.refs_1_
  7.4 0.2 convert_reduce_fusion
  7.7 1.6 %collective-permute-start.1 = (bf16[16,8192]{1,0:T(8,128)(2,1)S(1)}, bf16[16,8192]{1,0:T(8,128)(2,1)S(1)}, u32[]{:S(2)}, u32[]{:S(2)}) collective-permute-start(bf16[16,8192]{1,0:T(8,128)(2,1)S(1)} %collective-permute-done.refs_1_), channel_id=1, source_target_pairs={{0,2},{2,4},{4,6},{6,7},{7,5},{5,3},{3,1},{1,0},{8,9},{10,8},{12,1... | collective-permute-start | bytes 786440 | tf_op jit(solution)/shard_map/ppermute | solution.py:359
  9.4 1.6 %collective-permute-start.6 = (bf16[16,8192]{1,0:T(8,128)(2,1)S(1)}, bf16[16,8192]{1,0:T(8,128)(2,1)S(1)}, u32[]{:S(2)}, u32[]{:S(2)}) collective-permute-start(bf16[16,8192]{1,0:T(8,128)(2,1)S(1)} %collective-permute-done.5.refs_2_), channel_id=1, source_target_pairs={{0,2},{2,4},{4,6},{6,7},{7,5},{5,3},{3,1},{1,0},{8,9},{10,8},{12,1... | collective-permute-start | bytes 786440 | tf_op jit(solution)/shard_map/ppermute | solution.py:359
  11.0 3.2 %collective-permute-done.1.refs_4_ = bf16[16,8192]{1,0:T(8,128)(2,1)S(1)} collective-permute-done((bf16[16,8192]{1,0:T(8,128)(2,1)S(1)}, bf16[16,8192]{1,0:T(8,128)(2,1)S(1)}, u32[]{:S(2)}, u32[]{:S(2)}) %collective-permute-start.1) | collective-permute-done | bytes 262176 | tf_op jit(solution)/shard_map/ppermute | solution.py:359
  14.2 1.6 %collective-permute-start.2 = (bf16[16,8192]{1,0:T(8,128)(2,1)S(1)}, bf16[16,8192]{1,0:T(8,128)(2,1)S(1)}, u32[]{:S(2)}, u32[]{:S(2)}) collective-permute-start(bf16[16,8192]{1,0:T(8,128)(2,1)S(1)} %collective-permute-done.1.refs_4_), channel_id=1, source_target_pairs={{0,2},{2,4},{4,6},{6,7},{7,5},{5,3},{3,1},{1,0},{8,9},{10,8},{12,1... | collective-permute-start | bytes 786440 | tf_op jit(solution)/shard_map/ppermute | solution.py:359
  15.7 1.2 %collective-permute-done.6.refs_6_ = bf16[16,8192]{1,0:T(8,128)(2,1)S(1)} collective-permute-done((bf16[16,8192]{1,0:T(8,128)(2,1)S(1)}, bf16[16,8192]{1,0:T(8,128)(2,1)S(1)}, u32[]{:S(2)}, u32[]{:S(2)}) %collective-permute-start.6) | collective-permute-done | bytes 262176 | tf_op jit(solution)/shard_map/ppermute | solution.py:359
  17.0 1.6 %collective-permute-start.7 = (bf16[16,8192]{1,0:T(8,128)(2,1)S(1)}, bf16[16,8192]{1,0:T(8,128)(2,1)S(1)}, u32[]{:S(2)}, u32[]{:S(2)}) collective-permute-start(bf16[16,8192]{1,0:T(8,128)(2,1)S(1)} %collective-permute-done.6.refs_6_), channel_id=1, source_target_pairs={{0,2},{2,4},{4,6},{6,7},{7,5},{5,3},{3,1},{1,0},{8,9},{10,8},{12,1... | collective-permute-start | bytes 786440 | tf_op jit(solution)/shard_map/ppermute | solution.py:359
  18.6 0.5 collective-permute-start.11
  19.1 1.5 %collective-permute-done.2.refs_8_ = bf16[16,8192]{1,0:T(8,128)(2,1)S(1)} collective-permute-done((bf16[16,8192]{1,0:T(8,128)(2,1)S(1)}, bf16[16,8192]{1,0:T(8,128)(2,1)S(1)}, u32[]{:S(2)}, u32[]{:S(2)}) %collective-permute-start.2) | collective-permute-done | bytes 262176 | tf_op jit(solution)/shard_map/ppermute | solution.py:359
  20.5 1.6 %collective-permute-start.3 = (bf16[16,8192]{1,0:T(8,128)(2,1)S(1)}, bf16[16,8192]{1,0:T(8,128)(2,1)S(1)}, u32[]{:S(2)}, u32[]{:S(2)}) collective-permute-start(bf16[16,8192]{1,0:T(8,128)(2,1)S(1)} %collective-permute-done.2.refs_8_), channel_id=1, source_target_pairs={{0,2},{2,4},{4,6},{6,7},{7,5},{5,3},{3,1},{1,0},{8,9},{10,8},{12,1... | collective-permute-start | bytes 786440 | tf_op jit(solution)/shard_map/ppermute | solution.py:359
  22.1 1.2 %collective-permute-done.7.refs_10_ = bf16[16,8192]{1,0:T(8,128)(2,1)S(1)} collective-permute-done((bf16[16,8192]{1,0:T(8,128)(2,1)S(1)}, bf16[16,8192]{1,0:T(8,128)(2,1)S(1)}, u32[]{:S(2)}, u32[]{:S(2)}) %collective-permute-start.7) | collective-permute-done | bytes 262176 | tf_op jit(solution)/shard_map/ppermute | solution.py:359
  23.3 1.6 %collective-permute-start.8 = (bf16[16,8192]{1,0:T(8,128)(2,1)S(1)}, bf16[16,8192]{1,0:T(8,128)(2,1)S(1)}, u32[]{:S(2)}, u32[]{:S(2)}) collective-permute-start(bf16[16,8192]{1,0:T(8,128)(2,1)S(1)} %collective-permute-done.7.refs_10_), channel_id=1, source_target_pairs={{0,2},{2,4},{4,6},{6,7},{7,5},{5,3},{3,1},{1,0},{8,9},{10,8},{12,1... | collective-permute-start | bytes 786440 | tf_op jit(solution)/shard_map/ppermute | solution.py:359
  24.9 0.5 collective-permute-start.13
  25.5 1.4 %collective-permute-done.3.refs_0_ = bf16[16,8192]{1,0:T(8,128)(2,1)S(1)} collective-permute-done((bf16[16,8192]{1,0:T(8,128)(2,1)S(1)}, bf16[16,8192]{1,0:T(8,128)(2,1)S(1)}, u32[]{:S(2)}, u32[]{:S(2)}) %collective-permute-start.3) | collective-permute-done | bytes 262176 | tf_op jit(solution)/shard_map/ppermute | solution.py:359
  26.9 2.8 %collective-permute-done.8.refs_2_ = bf16[16,8192]{1,0:T(8,128)(2,1)S(1)} collective-permute-done((bf16[16,8192]{1,0:T(8,128)(2,1)S(1)}, bf16[16,8192]{1,0:T(8,128)(2,1)S(1)}, u32[]{:S(2)}, u32[]{:S(2)}) %collective-permute-start.8) | collective-permute-done | bytes 262176 | tf_op jit(solution)/shard_map/ppermute | solution.py:359
  29.7 1.7 %shard_map.91 = (bf16[2048,512]{1,0:T(8,128)(2,1)S(1)}, bf16[2048,128]{1,0:T(8,128)(2,1)S(1)}) custom-call(bf16[8192,512]{1,0:T(8,128)(2,1)} %refs_0_.7, bf16[8192,128]{1,0:T(8,128)(2,1)} %refs_1_.7), custom_call_target="tpu_custom_call" | custom-call | bytes 5242880 | tf_op jit(solution)/shard_map/pallas_call | solution.py:73
  31.4 1.7 %shard_map.92 = (bf16[2048,512]{1,0:T(8,128)(2,1)S(1)}, bf16[2048,128]{1,0:T(8,128)(2,1)S(1)}) custom-call(bf16[8192,512]{1,0:T(8,128)(2,1)} %refs_0_.7, bf16[8192,128]{1,0:T(8,128)(2,1)} %refs_1_.7), custom_call_target="tpu_custom_call" | custom-call | bytes 5242880 | tf_op jit(solution)/shard_map/pallas_call | solution.py:73
  33.1 1.7 %shard_map.93 = (bf16[2048,512]{1,0:T(8,128)(2,1)S(1)}, bf16[2048,128]{1,0:T(8,128)(2,1)S(1)}) custom-call(bf16[8192,512]{1,0:T(8,128)(2,1)} %refs_0_.7, bf16[8192,128]{1,0:T(8,128)(2,1)} %refs_1_.7), custom_call_target="tpu_custom_call" | custom-call | bytes 5242880 | tf_op jit(solution)/shard_map/pallas_call | solution.py:73
  34.8 1.7 %shard_map.94 = (bf16[2048,512]{1,0:T(8,128)(2,1)S(1)}, bf16[2048,128]{1,0:T(8,128)(2,1)S(1)}) custom-call(bf16[8192,512]{1,0:T(8,128)(2,1)} %refs_0_.7, bf16[8192,128]{1,0:T(8,128)(2,1)} %refs_1_.7), custom_call_target="tpu_custom_call" | custom-call | bytes 5242880 | tf_op jit(solution)/shard_map/pallas_call | solution.py:73
  36.6 2.6 %shard_map.95.refs_13_ = bf16[192,640]{1,0:T(8,128)(2,1)S(1)} custom-call(bf16[16,8192]{1,0:T(8,128)(2,1)S(1)} %norm.1.refs_0_, bf16[16,8192]{1,0:T(8,128)(2,1)S(1)} %collective-permute-done.refs_1_, bf16[16,8192]{1,0:T(8,128)(2,1)S(1)} %collective-permute-done.5.refs_2_, bf16[16,8192]{1,0:T(8,128)(2,1)S(1)} %collective-permute-done.10.refs_3_, ...), custom_call_target="tpu_custom_call" | custom-call | tf_op jit(solution)/shard_map/pallas_call | solution.py:127
  39.2 2.1 %shard_map.96 = bf16[256,640]{1,0:T(8,128)(2,1)S(1)} custom-call(bf16[16,8192]{1,0:T(8,128)(2,1)S(1)} %collective-permute-done.3.refs_0_, bf16[16,8192]{1,0:T(8,128)(2,1)S(1)} %collective-permute-done.4.refs_1_, bf16[16,8192]{1,0:T(8,128)(2,1)S(1)} %collective-permute-done.8.refs_2_, bf16[16,8192]{1,0:T(8,128)(2,1)S(1)} %collective-permute-done.9.refs_3_, ...), custom_call_target="tpu_custom_call" | custom-call | tf_op jit(solution)/shard_map/pallas_call | solution.py:127
  41.3 16.5 %all_to_all.22 = bf16[16,16,640]{2,1,0:T(8,128)(2,1)S(1)} all-to-all(bf16[16,16,640]{2,1,0:T(8,128)(2,1)S(1)} %bitcast.26), channel_id=1, replica_groups=mesh['groups'=2,'pool'=2,'tensor'=8] {'pool','tensor'}, dimensions={0} | all-to-all | bytes 655360 | tf_op jit(solution)/shard_map/all_to_all | solution.py:426
  57.8 5.1 %attend.1 = bf16[256,512]{1,0:T(8,128)(2,1)S(1)} custom-call(s32[16]{0:T(128)S(1)} %select_reduce_fusion.5.refs_0_, s32[16]{0:T(128)S(1)} %select_reduce_fusion.4.refs_1_, bf16[256,640]{1,0:T(8,128)(2,1)S(1)} %bitcast.27, bf16[16,256,1024]{2,1,0:T(8,128)(2,1)} %refs_3_.1, bf16[16,256,1024]{2,1,0:T(8,128)(2,1)} %refs_4_.1), custom_call_target="tpu_custom_call" | custom-call | tf_op jit(solution)/shard_map/attend/pallas_call | solution.py:258
  62.9 13.7 %all_to_all.23 = bf16[16,16,512]{2,1,0:T(8,128)(2,1)S(1)} all-to-all(bf16[16,16,512]{2,1,0:T(8,128)(2,1)S(1)} %bitcast.28), channel_id=1, replica_groups=mesh['groups'=2,'pool'=2,'tensor'=8] {'pool','tensor'}, dimensions={0} | all-to-all | bytes 524288 | tf_op jit(solution)/shard_map/all_to_all | solution.py:429
  76.7 3.8 %shard_map.97 = (bf16[48,8192]{1,0:T(8,128)(2,1)S(1)}, bf16[80,8192]{1,0:T(8,128)(2,1)S(1)}, bf16[512,8192]{1,0:T(8,128)(2,1)S(1)}) custom-call(s32[1,128]{1,0:T(1,128)S(1)} %reshape_reshape.13.refs_0_, bf16[256,512]{1,0:T(8,128)(2,1)S(1)} %bitcast.23, bf16[512,8192]{1,0:T(8,128)(2,1)} %refs_2_.1), custom_call_target="tpu_custom_call" | custom-call | tf_op jit(solution)/shard_map/pallas_call | solution.py:317
  80.6 0.5 collective-permute-start.16
  81.1 1.7 %shard_map.99.refs_0_.refs_2_ = bf16[48,8192]{1,0:T(8,128)(2,1)S(1)} custom-call(s32[1,48]{1,0:T(1,128)S(1)} %reshape_reshape.14.refs_0_, bf16[256,512]{1,0:T(8,128)(2,1)S(1)} %bitcast.24, bf16[512,8192]{1,0:T(8,128)(2,1)S(1)} %get-tuple-element.39.refs_2_), custom_call_target="tpu_custom_call" | custom-call | tf_op jit(solution)/shard_map/pallas_call | solution.py:317
  82.8 1.9 %collective-permute-done.16.refs_1_.refs_3_ = bf16[48,8192]{1,0:T(8,128)(2,1)S(1)} collective-permute-done((bf16[48,8192]{1,0:T(8,128)(2,1)S(1)}, bf16[48,8192]{1,0:T(8,128)(2,1)S(1)}, u32[]{:S(2)}, u32[]{:S(2)}) %collective-permute-start.16) | collective-permute-done | bytes 786464 | tf_op jit(solution)/shard_map/ppermute | solution.py:360
  84.9 0.8 collective-permute-start.17
  85.7 1.7 %shard_map.98.refs_0_ = bf16[80,8192]{1,0:T(8,128)(2,1)S(1)} custom-call(s32[1,80]{1,0:T(1,128)S(1)} %reshape_reshape.15.refs_0_, bf16[256,512]{1,0:T(8,128)(2,1)S(1)} %bitcast.25, bf16[512,8192]{1,0:T(8,128)(2,1)S(1)} %get-tuple-element.39.refs_2_), custom_call_target="tpu_custom_call" | custom-call | tf_op jit(solution)/shard_map/pallas_call | solution.py:317
  87.5 3.8 %collective-permute-done.17.refs_2_ = bf16[16,8192]{1,0:T(8,128)(2,1)S(1)} collective-permute-done((bf16[16,8192]{1,0:T(8,128)(2,1)S(1)}, bf16[16,8192]{1,0:T(8,128)(2,1)S(1)}, u32[]{:S(2)}, u32[]{:S(2)}) %collective-permute-start.17) | collective-permute-done | bytes 262176 | tf_op jit(solution)/shard_map/ppermute | solution.py:359
  91.4 0.8 collective-permute-start.18
  92.2 1.9 %collective-permute-done.21.refs_2_ = bf16[16,8192]{1,0:T(8,128)(2,1)S(1)} collective-permute-done((bf16[16,8192]{1,0:T(8,128)(2,1)S(1)}, bf16[16,8192]{1,0:T(8,128)(2,1)S(1)}, u32[]{:S(2)}, u32[]{:S(2)}) %collective-permute-start.21) | collective-permute-done | bytes 262176 | tf_op jit(solution)/shard_map/ppermute | solution.py:359
  94.2 0.8 collective-permute-start.22
  95.0 2.8 %collective-permute-done.18.refs_2_ = bf16[16,8192]{1,0:T(8,128)(2,1)S(1)} collective-permute-done((bf16[16,8192]{1,0:T(8,128)(2,1)S(1)}, bf16[16,8192]{1,0:T(8,128)(2,1)S(1)}, u32[]{:S(2)}, u32[]{:S(2)}) %collective-permute-start.18) | collective-permute-done | bytes 262176 | tf_op jit(solution)/shard_map/ppermute | solution.py:359
  97.9 0.8 collective-permute-start.19
  98.7 1.9 %collective-permute-done.22.refs_2_ = bf16[16,8192]{1,0:T(8,128)(2,1)S(1)} collective-permute-done((bf16[16,8192]{1,0:T(8,128)(2,1)S(1)}, bf16[16,8192]{1,0:T(8,128)(2,1)S(1)}, u32[]{:S(2)}, u32[]{:S(2)}) %collective-permute-start.22) | collective-permute-done | bytes 262176 | tf_op jit(solution)/shard_map/ppermute | solution.py:359
  100.7 0.8 collective-permute-start.23
  101.5 2.8 %collective-permute-done.19.refs_2_ = bf16[16,8192]{1,0:T(8,128)(2,1)S(1)} collective-permute-done((bf16[16,8192]{1,0:T(8,128)(2,1)S(1)}, bf16[16,8192]{1,0:T(8,128)(2,1)S(1)}, u32[]{:S(2)}, u32[]{:S(2)}) %collective-permute-start.19) | collective-permute-done | bytes 262176 | tf_op jit(solution)/shard_map/ppermute | solution.py:359
  104.4 0.8 collective-permute-start.20
  105.2 1.9 %collective-permute-done.23 = bf16[16,8192]{1,0:T(8,128)(2,1)S(1)} collective-permute-done((bf16[16,8192]{1,0:T(8,128)(2,1)S(1)}, bf16[16,8192]{1,0:T(8,128)(2,1)S(1)}, u32[]{:S(2)}, u32[]{:S(2)}) %collective-permute-start.23) | collective-permute-done | bytes 262176 | tf_op jit(solution)/shard_map/ppermute | solution.py:359
  107.2 3.7 %collective-permute-done.20.refs_2_ = bf16[16,8192]{1,0:T(8,128)(2,1)S(1)} collective-permute-done((bf16[16,8192]{1,0:T(8,128)(2,1)S(1)}, bf16[16,8192]{1,0:T(8,128)(2,1)S(1)}, u32[]{:S(2)}, u32[]{:S(2)}) %collective-permute-start.20) | collective-permute-done | bytes 262176 | tf_op jit(solution)/shard_map/ppermute | solution.py:359
  110.9 0.8 shard_map.106
  (43 shorter events, 2.3 us)
Async XLA Ops:
  1.2 6.5 %collective-permute-start = (bf16[16,8192]{1,0:T(8,128)(2,1)S(1)}, bf16[16,8192]{1,0:T(8,128)(2,1)S(1)}, u32[]{:S(2)}, u32[]{:S(2)}) collective-permute-start(bf16[16,8192]{1,0:T(8,128)(2,1)S(1)} %norm.1.refs_0_), channel_id=1, source_target_pairs={{0,8},{1,9},{2,10},{3,11},{4,12},{5,13},{6,14},{7,15},{8,0},{9,1},... | collective-permute-start | bytes 786440 | tf_op jit(solution)/shard_map/ppermute | solution.py:360
  1.7 7.6 %collective-permute-start.5 = (bf16[16,8192]{1,0:T(8,128)(2,1)S(1)}, bf16[16,8192]{1,0:T(8,128)(2,1)S(1)}, u32[]{:S(2)}, u32[]{:S(2)}) collective-permute-start(bf16[16,8192]{1,0:T(8,128)(2,1)S(1)} %norm.1.refs_0_), channel_id=1, source_target_pairs={{0,2},{2,4},{4,6},{6,7},{7,5},{5,3},{3,1},{1,0},{8,9},{10,8},{12,1... | collective-permute-start | bytes 786440 | tf_op jit(solution)/shard_map/ppermute | solution.py:359
  7.7 6.4 %collective-permute-start.1 = (bf16[16,8192]{1,0:T(8,128)(2,1)S(1)}, bf16[16,8192]{1,0:T(8,128)(2,1)S(1)}, u32[]{:S(2)}, u32[]{:S(2)}) collective-permute-start(bf16[16,8192]{1,0:T(8,128)(2,1)S(1)} %collective-permute-done.refs_1_), channel_id=1, source_target_pairs={{0,2},{2,4},{4,6},{6,7},{7,5},{5,3},{3,1},{1,0},{8,9},{10,8},{12,1... | collective-permute-start | bytes 786440 | tf_op jit(solution)/shard_map/ppermute | solution.py:359
  9.4 7.6 %collective-permute-start.6 = (bf16[16,8192]{1,0:T(8,128)(2,1)S(1)}, bf16[16,8192]{1,0:T(8,128)(2,1)S(1)}, u32[]{:S(2)}, u32[]{:S(2)}) collective-permute-start(bf16[16,8192]{1,0:T(8,128)(2,1)S(1)} %collective-permute-done.5.refs_2_), channel_id=1, source_target_pairs={{0,2},{2,4},{4,6},{6,7},{7,5},{5,3},{3,1},{1,0},{8,9},{10,8},{12,1... | collective-permute-start | bytes 786440 | tf_op jit(solution)/shard_map/ppermute | solution.py:359
  14.2 6.4 %collective-permute-start.2 = (bf16[16,8192]{1,0:T(8,128)(2,1)S(1)}, bf16[16,8192]{1,0:T(8,128)(2,1)S(1)}, u32[]{:S(2)}, u32[]{:S(2)}) collective-permute-start(bf16[16,8192]{1,0:T(8,128)(2,1)S(1)} %collective-permute-done.1.refs_4_), channel_id=1, source_target_pairs={{0,2},{2,4},{4,6},{6,7},{7,5},{5,3},{3,1},{1,0},{8,9},{10,8},{12,1... | collective-permute-start | bytes 786440 | tf_op jit(solution)/shard_map/ppermute | solution.py:359
  17.0 6.4 %collective-permute-start.7 = (bf16[16,8192]{1,0:T(8,128)(2,1)S(1)}, bf16[16,8192]{1,0:T(8,128)(2,1)S(1)}, u32[]{:S(2)}, u32[]{:S(2)}) collective-permute-start(bf16[16,8192]{1,0:T(8,128)(2,1)S(1)} %collective-permute-done.6.refs_6_), channel_id=1, source_target_pairs={{0,2},{2,4},{4,6},{6,7},{7,5},{5,3},{3,1},{1,0},{8,9},{10,8},{12,1... | collective-permute-start | bytes 786440 | tf_op jit(solution)/shard_map/ppermute | solution.py:359
  18.6 6.4 %collective-permute-start.10 = (bf16[16,8192]{1,0:T(8,128)(2,1)S(1)}, bf16[16,8192]{1,0:T(8,128)(2,1)S(1)}, u32[]{:S(2)}, u32[]{:S(2)}) collective-permute-start(bf16[16,8192]{1,0:T(8,128)(2,1)S(1)} %collective-permute-done.5.refs_2_), channel_id=1, source_target_pairs={{0,8},{1,9},{2,10},{3,11},{4,12},{5,13},{6,14},{7,15},{8,0},{9,1},... | collective-permute-start | bytes 786440 | tf_op jit(solution)/shard_map/ppermute | solution.py:360
  18.6 6.9 %collective-permute-start.11 = (bf16[16,8192]{1,0:T(8,128)(2,1)S(1)}, bf16[16,8192]{1,0:T(8,128)(2,1)S(1)}, u32[]{:S(2)}, u32[]{:S(2)}) collective-permute-start(bf16[16,8192]{1,0:T(8,128)(2,1)S(1)} %collective-permute-done.1.refs_4_), channel_id=1, source_target_pairs={{0,8},{1,9},{2,10},{3,11},{4,12},{5,13},{6,14},{7,15},{8,0},{9,1},... | collective-permute-start | bytes 786440 | tf_op jit(solution)/shard_map/ppermute | solution.py:360
  20.5 6.4 %collective-permute-start.3 = (bf16[16,8192]{1,0:T(8,128)(2,1)S(1)}, bf16[16,8192]{1,0:T(8,128)(2,1)S(1)}, u32[]{:S(2)}, u32[]{:S(2)}) collective-permute-start(bf16[16,8192]{1,0:T(8,128)(2,1)S(1)} %collective-permute-done.2.refs_8_), channel_id=1, source_target_pairs={{0,2},{2,4},{4,6},{6,7},{7,5},{5,3},{3,1},{1,0},{8,9},{10,8},{12,1... | collective-permute-start | bytes 786440 | tf_op jit(solution)/shard_map/ppermute | solution.py:359
  23.3 6.4 %collective-permute-start.8 = (bf16[16,8192]{1,0:T(8,128)(2,1)S(1)}, bf16[16,8192]{1,0:T(8,128)(2,1)S(1)}, u32[]{:S(2)}, u32[]{:S(2)}) collective-permute-start(bf16[16,8192]{1,0:T(8,128)(2,1)S(1)} %collective-permute-done.7.refs_10_), channel_id=1, source_target_pairs={{0,2},{2,4},{4,6},{6,7},{7,5},{5,3},{3,1},{1,0},{8,9},{10,8},{12,1... | collective-permute-start | bytes 786440 | tf_op jit(solution)/shard_map/ppermute | solution.py:359
  24.9 11.6 %collective-permute-start.12 = (bf16[16,8192]{1,0:T(8,128)(2,1)S(1)}, bf16[16,8192]{1,0:T(8,128)(2,1)S(1)}, u32[]{:S(2)}, u32[]{:S(2)}) collective-permute-start(bf16[16,8192]{1,0:T(8,128)(2,1)S(1)} %collective-permute-done.6.refs_6_), channel_id=1, source_target_pairs={{0,8},{1,9},{2,10},{3,11},{4,12},{5,13},{6,14},{7,15},{8,0},{9,1},... | collective-permute-start | bytes 786440 | tf_op jit(solution)/shard_map/ppermute | solution.py:360
  24.9 11.6 %collective-permute-start.13 = (bf16[16,8192]{1,0:T(8,128)(2,1)S(1)}, bf16[16,8192]{1,0:T(8,128)(2,1)S(1)}, u32[]{:S(2)}, u32[]{:S(2)}) collective-permute-start(bf16[16,8192]{1,0:T(8,128)(2,1)S(1)} %collective-permute-done.2.refs_8_), channel_id=1, source_target_pairs={{0,8},{1,9},{2,10},{3,11},{4,12},{5,13},{6,14},{7,15},{8,0},{9,1},... | collective-permute-start | bytes 786440 | tf_op jit(solution)/shard_map/ppermute | solution.py:360
  25.4 11.1 %collective-permute-start.14 = (bf16[16,8192]{1,0:T(8,128)(2,1)S(1)}, bf16[16,8192]{1,0:T(8,128)(2,1)S(1)}, u32[]{:S(2)}, u32[]{:S(2)}) collective-permute-start(bf16[16,8192]{1,0:T(8,128)(2,1)S(1)} %collective-permute-done.7.refs_10_), channel_id=1, source_target_pairs={{0,8},{1,9},{2,10},{3,11},{4,12},{5,13},{6,14},{7,15},{8,0},{9,1},... | collective-permute-start | bytes 786440 | tf_op jit(solution)/shard_map/ppermute | solution.py:360
  26.9 12.3 %collective-permute-start.4 = (bf16[16,8192]{1,0:T(8,128)(2,1)S(1)}, bf16[16,8192]{1,0:T(8,128)(2,1)S(1)}, u32[]{:S(2)}, u32[]{:S(2)}) collective-permute-start(bf16[16,8192]{1,0:T(8,128)(2,1)S(1)} %collective-permute-done.3.refs_0_), channel_id=1, source_target_pairs={{0,8},{1,9},{2,10},{3,11},{4,12},{5,13},{6,14},{7,15},{8,0},{9,1},... | collective-permute-start | bytes 786440 | tf_op jit(solution)/shard_map/ppermute | solution.py:360
  29.7 9.5 %collective-permute-start.9 = (bf16[16,8192]{1,0:T(8,128)(2,1)S(1)}, bf16[16,8192]{1,0:T(8,128)(2,1)S(1)}, u32[]{:S(2)}, u32[]{:S(2)}) collective-permute-start(bf16[16,8192]{1,0:T(8,128)(2,1)S(1)} %collective-permute-done.8.refs_2_), channel_id=1, source_target_pairs={{0,8},{1,9},{2,10},{3,11},{4,12},{5,13},{6,14},{7,15},{8,0},{9,1},... | collective-permute-start | bytes 786440 | tf_op jit(solution)/shard_map/ppermute | solution.py:360
  80.5 13.6 %collective-permute-start.15 = (bf16[80,8192]{1,0:T(8,128)(2,1)S(1)}, bf16[80,8192]{1,0:T(8,128)(2,1)S(1)}, u32[]{:S(2)}, u32[]{:S(2)}) collective-permute-start(bf16[80,8192]{1,0:T(8,128)(2,1)S(1)} %get-tuple-element.40), channel_id=1, source_target_pairs={{0,8},{1,9},{2,10},{3,11},{4,12},{5,13},{6,14},{7,15},{8,0},{9,1},... | collective-permute-start | bytes 3932168 | tf_op jit(solution)/shard_map/ppermute | solution.py:360
  80.6 4.1 %collective-permute-start.16 = (bf16[48,8192]{1,0:T(8,128)(2,1)S(1)}, bf16[48,8192]{1,0:T(8,128)(2,1)S(1)}, u32[]{:S(2)}, u32[]{:S(2)}) collective-permute-start(bf16[48,8192]{1,0:T(8,128)(2,1)S(1)} %get-tuple-element.42), channel_id=1, source_target_pairs={{0,8},{1,9},{2,10},{3,11},{4,12},{5,13},{6,14},{7,15},{8,0},{9,1},... | collective-permute-start | bytes 2359304 | tf_op jit(solution)/shard_map/ppermute | solution.py:360
  84.9 6.4 %collective-permute-start.17 = (bf16[16,8192]{1,0:T(8,128)(2,1)S(1)}, bf16[16,8192]{1,0:T(8,128)(2,1)S(1)}, u32[]{:S(2)}, u32[]{:S(2)}) collective-permute-start(bf16[16,8192]{1,0:T(8,128)(2,1)S(1)} %get-tuple-element.43), channel_id=1, source_target_pairs={{0,2},{2,4},{4,6},{6,7},{7,5},{5,3},{3,1},{1,0},{8,9},{10,8},{12,1... | collective-permute-start | bytes 786440 | tf_op jit(solution)/shard_map/ppermute | solution.py:359
  85.7 8.4 %collective-permute-start.21 = (bf16[16,8192]{1,0:T(8,128)(2,1)S(1)}, bf16[16,8192]{1,0:T(8,128)(2,1)S(1)}, u32[]{:S(2)}, u32[]{:S(2)}) collective-permute-start(bf16[16,8192]{1,0:T(8,128)(2,1)S(1)} %get-tuple-element.44), channel_id=1, source_target_pairs={{0,2},{2,4},{4,6},{6,7},{7,5},{5,3},{3,1},{1,0},{8,9},{10,8},{12,1... | collective-permute-start | bytes 786440 | tf_op jit(solution)/shard_map/ppermute | solution.py:359
  91.4 6.4 %collective-permute-start.18 = (bf16[16,8192]{1,0:T(8,128)(2,1)S(1)}, bf16[16,8192]{1,0:T(8,128)(2,1)S(1)}, u32[]{:S(2)}, u32[]{:S(2)}) collective-permute-start(bf16[16,8192]{1,0:T(8,128)(2,1)S(1)} %shard_map.101), channel_id=1, source_target_pairs={{0,2},{2,4},{4,6},{6,7},{7,5},{5,3},{3,1},{1,0},{8,9},{10,8},{12,1... | collective-permute-start | bytes 786440 | tf_op jit(solution)/shard_map/ppermute | solution.py:359
  94.2 6.4 %collective-permute-start.22 = (bf16[16,8192]{1,0:T(8,128)(2,1)S(1)}, bf16[16,8192]{1,0:T(8,128)(2,1)S(1)}, u32[]{:S(2)}, u32[]{:S(2)}) collective-permute-start(bf16[16,8192]{1,0:T(8,128)(2,1)S(1)} %shard_map.104), channel_id=1, source_target_pairs={{0,2},{2,4},{4,6},{6,7},{7,5},{5,3},{3,1},{1,0},{8,9},{10,8},{12,1... | collective-permute-start | bytes 786440 | tf_op jit(solution)/shard_map/ppermute | solution.py:359
  97.9 6.4 %collective-permute-start.19 = (bf16[16,8192]{1,0:T(8,128)(2,1)S(1)}, bf16[16,8192]{1,0:T(8,128)(2,1)S(1)}, u32[]{:S(2)}, u32[]{:S(2)}) collective-permute-start(bf16[16,8192]{1,0:T(8,128)(2,1)S(1)} %shard_map.102), channel_id=1, source_target_pairs={{0,2},{2,4},{4,6},{6,7},{7,5},{5,3},{3,1},{1,0},{8,9},{10,8},{12,1... | collective-permute-start | bytes 786440 | tf_op jit(solution)/shard_map/ppermute | solution.py:359
  100.7 6.4 %collective-permute-start.23 = (bf16[16,8192]{1,0:T(8,128)(2,1)S(1)}, bf16[16,8192]{1,0:T(8,128)(2,1)S(1)}, u32[]{:S(2)}, u32[]{:S(2)}) collective-permute-start(bf16[16,8192]{1,0:T(8,128)(2,1)S(1)} %shard_map.105), channel_id=1, source_target_pairs={{0,2},{2,4},{4,6},{6,7},{7,5},{5,3},{3,1},{1,0},{8,9},{10,8},{12,1... | collective-permute-start | bytes 786440 | tf_op jit(solution)/shard_map/ppermute | solution.py:359
  104.4 6.4 %collective-permute-start.20 = (bf16[16,8192]{1,0:T(8,128)(2,1)S(1)}, bf16[16,8192]{1,0:T(8,128)(2,1)S(1)}, u32[]{:S(2)}, u32[]{:S(2)}) collective-permute-start(bf16[16,8192]{1,0:T(8,128)(2,1)S(1)} %shard_map.103), channel_id=1, source_target_pairs={{0,2},{2,4},{4,6},{6,7},{7,5},{5,3},{3,1},{1,0},{8,9},{10,8},{12,1... | collective-permute-start | bytes 786440 | tf_op jit(solution)/shard_map/ppermute | solution.py:359
  107.2 3.7 %collective-permute-start.24 = (bf16[16,8192]{1,0:T(8,128)(2,1)S(1)}, bf16[16,8192]{1,0:T(8,128)(2,1)S(1)}, u32[]{:S(2)}, u32[]{:S(2)}) collective-permute-start(bf16[16,8192]{1,0:T(8,128)(2,1)S(1)} %collective-permute-done.23), channel_id=1, source_target_pairs={{0,8},{1,9},{2,10},{3,11},{4,12},{5,13},{6,14},{7,15},{8,0},{9,1},... | collective-permute-start | bytes 786440 | tf_op jit(solution)/shard_map/ppermute | solution.py:360
